TPU v7x, 32 devices: a whole 2x2x4 slice. The times are simulated.
32 devices in a mesh: frame: 2 (over core), slab: 16 (over z, y, x).
Axes of the slice: x: 2, y: 2, z: 4, core: 2. Of those that a mesh axis runs over, the one named last changes fastest.
Arguments:
- volume: float32 [2, 1024, 8192], P('frame', 'slab'), may hold values from -6 to 6
- measured: float32 [2, 2, 1024, 8192], P('frame', None, None, 'slab'), may hold values from -6 to 6
- cutoff: int32 [2, 8192], P('frame', 'slab'), may hold values from 128 to 384
Outputs:
- smoothed: float32 [2, 1024, 8192], P('frame', 'slab')
All inputs are finite; a program needn't handle non-finite values.
Results may differ from a plain program's by a relative error of at most 0.0003.
Values sent between devices are 32-bit elements; how exact they have to be, the bound alone decides.
No kernel may reach another device: no remote copies, remote signals or barrier semaphores. Data moves between devices by JAX's collectives and lax.ppermute only.
A program may use at most 128 MiB of HBM per device.

v0:
```python
import math

import jax
import jax.numpy as jnp
from jax import lax
from jax.sharding import PartitionSpec as P

tv_step_size = 0.25
tv_weight = 1.0


def extended_2(block, sides, width):
    for axis, dim in sides:
        count = lax.axis_size(axis)
        forward = [(i, i + 1) for i in range(count - 1)]
        backward = [(target, source) for source, target in forward]
        low = lax.ppermute(
            lax.slice_in_dim(block, block.shape[dim] - width, None, axis=dim), axis, forward
        )
        high = lax.ppermute(lax.slice_in_dim(block, 0, width, axis=dim), axis, backward)
        block = jnp.concatenate([low, block, high], axis=dim)
    return block


def tv_step(extended, anchor, first_frame, frames):
    difference = extended[1:] - extended[:-1]
    frame_ids = first_frame + jnp.arange(difference.shape[0], dtype=jnp.int32)
    inside = ((frame_ids >= 0) & (frame_ids <= frames - 2))[:, None, None]
    fluxes = jnp.where(inside, difference / jnp.sqrt(difference * difference + 1.0), 0.0)
    interior = extended[1:-1]
    return interior - tv_step_size * (interior - anchor + tv_weight * (fluxes[:-1] - fluxes[1:]))


def tables(length):
    indices = jnp.arange(length, dtype=jnp.int32)
    product = indices[:, None] * indices[None, :] % length
    angle = product.astype(jnp.float32) * (2.0 * math.pi / length)
    scale = 1.0 / math.sqrt(length)
    return (jnp.cos(angle) * scale, jnp.sin(angle) * scale)


def back_to_slabs(columns):
    return lax.all_to_all(columns, "slab", split_axis=1, concat_axis=2, tiled=True)


def smooth(anchor, first_frame, frames):
    current = anchor
    for step in range(2):
        extended = extended_2(current, (("frame", 0),), 1)
        current = tv_step(extended, anchor, first_frame - 1, frames)
    return current


def on_device(volume, measured, cutoff):
    columns = lax.all_to_all(volume, "slab", split_axis=2, concat_axis=1, tiled=True)
    length = columns.shape[1]
    cos_table, sin_table = tables(length)
    highest = lax.Precision.HIGHEST
    local_frames = columns.shape[0]
    frames = lax.axis_size("frame") * local_frames
    first_frame = lax.axis_index("frame") * local_frames
    indices = jnp.arange(length, dtype=jnp.int32)
    signed = jnp.where(indices < length // 2, indices, indices - length)
    column_field = columns[0]
    real_part = jnp.dot(
        cos_table, column_field, precision=highest, preferred_element_type=jnp.float32
    )
    imag_part = -jnp.dot(
        sin_table, column_field, precision=highest, preferred_element_type=jnp.float32
    )
    measured_mask = jnp.abs(signed)[:, None] <= cutoff[0][None, :]
    real_part = jnp.where(measured_mask, measured[0, 0], real_part)
    imag_part = jnp.where(measured_mask, measured[0, 1], imag_part)
    restored = jnp.dot(cos_table, real_part, precision=highest, preferred_element_type=jnp.float32)
    restored = restored - jnp.dot(
        sin_table, imag_part, precision=highest, preferred_element_type=jnp.float32
    )
    restored_list = [restored]
    anchor = jnp.stack(restored_list, axis=0)
    slabs = back_to_slabs(anchor)
    return smooth(slabs, first_frame, frames)


def solution(mesh):
    placed = (P("frame", "slab", None), P("frame", None, None, "slab"), P("frame", "slab"))
    return jax.shard_map(
        on_device, mesh=mesh, in_specs=placed, out_specs=P("frame", "slab", None), check_vma=False
    )
```

profile of v0, /device:TPU:0, one launch (start us, length us, event | category | flops | bytes accessed | tf_op | source)
XLA Modules:
  0.0 303.0 jit_solution(15545078532024128834)
XLA Ops:
  0.0 9.2 %copy.8 = f32[1,64,8192]{1,0,2:T(1,128)} copy(f32[1,64,8192]{2,1,0:T(8,128)} %param.3) | data formatting | bytes 4194304 | tf_op args[0]
  9.7 38.4 %reduce = f32[8192,64]{1,0:T(8,128)} reduce(f32[8192,1,64]{2,1,0:T(1,128)} %bitcast.28, f32[]{:T(128)} %broadcast.86), dimensions={1}, to_apply=%bitcast.23.reduce_sub_computation | reduce | bytes 4194308
  48.1 5.5 %reshape.29 = f32[16,1,32768]{2,1,0:T(1,128)} reshape(f32[8192,64]{1,0:T(8,128)} %reduce) | data formatting | bytes 4194304
  53.6 8.6 %all-to-all-start = ((f32[16,1,32768]{2,1,0:T(1,128)}), f32[16,1,32768]{2,1,0:T(1,128)}, u32[]{:S(2)}, u32[]{:S(2)}) async-start(f32[16,1,32768]{2,1,0:T(1,128)} %reshape.29), calls=%async_computation | async-start | bytes 4194304 | tf_op jit(solution)/shard_map/all_to_all | solution.py:55
  62.2 43.0 %all-to-all-done = f32[16,1,32768]{2,1,0:T(1,128)} async-done(((f32[16,1,32768]{2,1,0:T(1,128)}), f32[16,1,32768]{2,1,0:T(1,128)}, u32[]{:S(2)}, u32[]{:S(2)}) %all-to-all-start) | async-done | bytes 2097184 | tf_op jit(solution)/shard_map/all_to_all | solution.py:55
  105.2 7.3 %reduce.1 = f32[16,32768]{1,0:T(8,128)S(1)} reduce(f32[16,1,32768]{2,1,0:T(1,128)} %all-to-all-done, f32[]{:T(128)} %broadcast.86), dimensions={1}, to_apply=%all_to_all.24.reduce_sub_computation | reduce | bytes 4194308 | tf_op jit(solution)/shard_map/all_to_all | solution.py:55
  112.5 6.6 %reshape.30 = f32[8192,1,64]{2,1,0:T(1,128)} reshape(f32[16,32768]{1,0:T(8,128)S(1)} %reduce.1) | data formatting | bytes 4194304
  119.0 3.8 %copy.13 = f32[1,64,16,512]{3,2,1,0:T(8,128)S(1)} copy(f32[1,64,16,512]{1,3,2,0:T(8,128)} %bitcast.27) | data formatting | bytes 4194304 | tf_op jit(solution)/shard_map/all_to_all | solution.py:55
  124.0 22.3 %fusion.9 = f32[1024,512]{1,0:T(8,128)S(1)} fusion(f32[1024,512]{1,0:T(8,128)S(1)} %bitcast.31), kind=kOutput, calls=%fused_computation.18 | convolution fusion | flops 6458179584 | bytes 4194304 | tf_op jit(solution)/shard_map/dot_general | solution.py:68
  146.4 22.6 %fusion.7 = f32[1024,512]{1,0:T(8,128)S(1)} fusion(f32[1024,512]{1,0:T(8,128)S(1)} %bitcast.32), kind=kOutput, calls=%fused_computation.16 | convolution fusion | flops 6458179584 | bytes 4194304 | tf_op jit(solution)/shard_map/dot_general | solution.py:65
  169.1 22.7 %fusion.6 = f32[1024,512]{1,0:T(8,128)S(1)} fusion(f32[1024,512]{1,0:T(8,128)S(1)} %fusion.7, f32[1,2,1024,512]{3,2,1,0:T(8,128)S(1)} %copy-done, s32[512]{0:T(512)S(1)} %bitcast.33, s32[1024]{0:T(1024)S(1)} %fusion.33), kind=kOutput, calls=%fused_computation.15 | convolution fusion | flops 6459228160 | bytes 6297600 | tf_op jit(solution)/shard_map/dot_general | solution.py:74
  191.8 23.6 %subtract_bitcast_fusion = f32[1,1024,512]{2,1,0:T(8,128)S(1)} fusion(f32[1024,512]{1,0:T(8,128)S(1)} %fusion.6, f32[1024,512]{1,0:T(8,128)S(1)} %fusion.9, f32[1,2,1024,512]{3,2,1,0:T(8,128)S(1)} %copy-done, s32[512]{0:T(512)S(1)} %bitcast.34, s32[1024]{0:T(1024)S(1)} %fusion.33), kind=kOutput, calls=%fused_computation.31 | convolution fusion | flops 6460276736 | bytes 8394752 | tf_op jit(solution)/shard_map/dot_general | solution.py:75
  215.3 2.2 copy.11
  217.5 58.0 %all_to_all.33 = f32[1,1024,512]{2,0,1:T(1,128)S(1)} all-to-all(f32[1,1024,512]{2,0,1:T(1,128)S(1)} %copy.11), channel_id=1, replica_groups=mesh['frame'=2,'slab'=16] {'slab'}, dimensions={1} | all-to-all | bytes 4194304 | tf_op jit(solution)/shard_map/all_to_all | solution.py:43
  275.5 2.5 copy.12
  278.0 1.7 all_to_all.30
  279.8 2.6 collective-permute-start.1
  285.0 3.6 %collective-permute-done = f32[1,64,8192]{2,1,0:T(8,128)} collective-permute-done((f32[1,64,8192]{2,1,0:T(8,128)S(1)}, f32[1,64,8192]{2,1,0:T(8,128)}, u32[]{:S(2)}, u32[]{:S(2)}) %collective-permute-start) | collective-permute-done | bytes 2097184 | tf_op jit(solution)/shard_map/ppermute | solution.py:20
  288.6 2.6 multiply_select_fusion.1
  291.6 2.2 collective-permute-start.3
  293.7 1.3 collective-permute-start.2
  295.0 2.3 collective-permute-done.3
  297.4 2.4 collective-permute-done.2
  300.7 1.9 fusion.12
  (12 shorter events, 5.5 us)
Async XLA Ops:
  53.6 51.6 %all-to-all-start = ((f32[16,1,32768]{2,1,0:T(1,128)}), f32[16,1,32768]{2,1,0:T(1,128)}, u32[]{:S(2)}, u32[]{:S(2)}) async-start(f32[16,1,32768]{2,1,0:T(1,128)} %reshape.29), calls=%async_computation | async-start | bytes 4194304 | tf_op jit(solution)/shard_map/all_to_all | solution.py:55
  146.4 22.7 %copy-start = (f32[1,2,1024,512]{3,2,1,0:T(8,128)S(1)}, f32[1,2,1024,512]{3,2,1,0:T(8,128)}, u32[]{:S(2)}) copy-start(f32[1,2,1024,512]{3,2,1,0:T(8,128)} %param.4) | copy-start | bytes 12582916
  146.4 22.7 %copy-start.1 = (s32[1,512]{1,0:T(1,128)S(1)}, s32[1,512]{1,0:T(1,128)}, u32[]{:S(2)}) copy-start(s32[1,512]{1,0:T(1,128)} %param.5) | copy-start | bytes 6148
  279.8 5.2 %collective-permute-start.1 = (f32[1,64,8192]{2,1,0:T(8,128)S(1)}, f32[1,64,8192]{2,1,0:T(8,128)}, u32[]{:S(2)}, u32[]{:S(2)}) collective-permute-start(f32[1,64,8192]{2,1,0:T(8,128)S(1)} %all_to_all.30), channel_id=1, source_target_pairs={{0,16},{1,17},{2,18},{3,19},{4,20},{5,21},{6,22},{7,23},{8,24},{9,... | collective-permute-start | bytes 6291464 | tf_op jit(solution)/shard_map/ppermute | solution.py:17
  282.4 6.2 %collective-permute-start = (f32[1,64,8192]{2,1,0:T(8,128)S(1)}, f32[1,64,8192]{2,1,0:T(8,128)}, u32[]{:S(2)}, u32[]{:S(2)}) collective-permute-start(f32[1,64,8192]{2,1,0:T(8,128)S(1)} %all_to_all.30), channel_id=1, source_target_pairs={{16,0},{17,1},{18,2},{19,3},{20,4},{21,5},{22,6},{23,7},{24,8},{25... | collective-permute-start | bytes 6291464 | tf_op jit(solution)/shard_map/ppermute | solution.py:20
  291.6 5.8 %collective-permute-start.3 = (f32[1,64,8192]{2,1,0:T(8,128)S(1)}, f32[1,64,8192]{2,1,0:T(8,128)S(1)}, u32[]{:S(2)}, u32[]{:S(2)}) collective-permute-start(f32[1,64,8192]{2,1,0:T(8,128)S(1)} %fusion.15), channel_id=1, source_target_pairs={{0,16},{1,17},{2,18},{3,19},{4,20},{5,21},{6,22},{7,23},{8,24},{9,... | collective-permute-start | bytes 6291464 | tf_op jit(solution)/shard_map/ppermute | solution.py:17
  293.7 6.1 %collective-permute-start.2 = (f32[1,64,8192]{2,1,0:T(8,128)S(1)}, f32[1,64,8192]{2,1,0:T(8,128)S(1)}, u32[]{:S(2)}, u32[]{:S(2)}) collective-permute-start(f32[1,64,8192]{2,1,0:T(8,128)S(1)} %fusion.15), channel_id=1, source_target_pairs={{16,0},{17,1},{18,2},{19,3},{20,4},{21,5},{22,6},{23,7},{24,8},{25... | collective-permute-start | bytes 6291464 | tf_op jit(solution)/shard_map/ppermute | solution.py:20
where the time goes:
time: 308 us; the launch traced here: 303 us
  matrix products  91.2 us (30%)
  blocking collectives  58 us (19%)
  waiting for transfers between devices  52.6 us (17%)
  other arithmetic  51.4 us (17%)
  local copies, waits for them, and re-layouts  33.2 us (11%)
  starting transfers between devices  16 us (5%)
    all_to_all x1, blocking collectives, back_to_slabs(): lax.all_to_all(columns, 'slab', split_axis=1, concat_axis=2, tiled=True)  58 us
    all_to_all x1, waiting for transfers between devices, on_device(): lax.all_to_all(volume, 'slab', split_axis=2, concat_axis=1, tiled=True)  43 us
    unnamed x1, other arithmetic  38.4 us
    dot_general x1, matrix products, on_device(): jnp.dot(sin_table, imag_part, precision=highest, preferred_element_type=j...  23.6 us
    dot_general x1, matrix products, on_device(): jnp.dot(cos_table, real_part, precision=highest, preferred_element_type=j...  22.7 us
    dot_general x1, matrix products, on_device(): jnp.dot(cos_table, column_field, precision=highest, preferred_element_typ...  22.6 us
    dot_general x1, matrix products, on_device(): jnp.dot(sin_table, column_field, precision=highest, preferred_element_typ...  22.3 us
    unnamed x8, local copies, waits for them, and re-layouts  21.8 us
  transfers between devices with their start and end apart: 5, of which 5 were waited for; matrix products, arithmetic and copies ran while one was open for 0% of the time, Pallas kernels for 0%

commit v1 on v0

v1 whole, which is shorter than its diff:
```python
import functools
import math

import jax
import jax.numpy as jnp
import numpy as np
from jax import lax
from jax.experimental import pallas as pl
from jax.experimental.pallas import tpu as pltpu
from jax.sharding import PartitionSpec as P

tv_step_size = 0.25
tv_weight = 1.0
EXTRA = 8


def split(array):
    high = array.astype(jnp.bfloat16)
    low = (array - high.astype(jnp.float32)).astype(jnp.bfloat16)
    return high, low


def product(table_high, table_low, array):
    high, low = split(array)
    dot = functools.partial(jnp.dot, preferred_element_type=jnp.float32)
    return dot(table_high[...], high) + (dot(table_high[...], low) + dot(table_low[...], high))


def as_pair(table):
    table = table.astype(np.float32)
    high = table.astype(jnp.bfloat16)
    low = (table - high.astype(np.float32)).astype(jnp.bfloat16)
    return [jnp.asarray(high), jnp.asarray(low)]


def rows(length, first, count):
    k = first + 2 * np.arange(count)
    z = np.arange(length // 2)
    angle = (k[:, None] * z[None, :] % length) * (2.0 * math.pi / length)
    table = np.concatenate([np.cos(angle), -np.sin(angle)], axis=0) / math.sqrt(length)
    return k, table


def band_tables(length):
    count = 3 * length // 16
    result = []
    for first in (length // 8 + 2, length // 8 + 1):
        k, table = rows(length, first, count)
        weight = np.where(k == length // 2, 1.0, 2.0)
        result += as_pair(table * np.concatenate([weight, weight])[:, None])
        result += as_pair(table.T)
    return result


def measured_tables(length):
    result = []
    for first in (0, 1):
        result += as_pair(rows(length, first, length // 2)[1].T)
    return result


def measured_kernel(measured, cutoff, even_high, even_low, odd_high, odd_low, out):
    length = measured.shape[1]
    half = length // 2
    limit = cutoff[...]
    parts = []
    for first, high, low in ((0, even_high, even_low), (1, odd_high, odd_low)):
        k = first + 2 * lax.broadcasted_iota(jnp.int32, (half, limit.shape[1]), 0)
        keep = jnp.where(k < half, k, length - k) <= limit
        stacked = [
            jnp.where(keep, measured[part, pl.ds(first, half, stride=2), :], 0.0) for part in (0, 1)
        ]
        parts.append(product(high, low, jnp.concatenate(stacked, axis=0)))
    out[:half, :] = parts[0] + parts[1]
    out[half:length, :] = parts[0] - parts[1]
    out[length:, :] = jnp.broadcast_to(limit.astype(jnp.float32), (EXTRA, limit.shape[1]))


def measured_part(measured, cutoff, tables):
    length, columns = measured.shape[1:]
    width = 128 if columns % 128 == 0 else columns
    whole = pl.BlockSpec(memory_space=pltpu.VMEM)
    return pl.pallas_call(
        measured_kernel,
        grid=(columns // width,),
        in_specs=[
            pl.BlockSpec((2, length, width), lambda i: (0, 0, i)),
            pl.BlockSpec((1, width), lambda i: (0, i)),
        ]
        + [whole] * len(tables),
        out_specs=pl.BlockSpec((length + EXTRA, width), lambda i: (0, i)),
        out_shape=jax.ShapeDtypeStruct((length + EXTRA, columns), jnp.float32),
        name="measured_part",
    )(measured, cutoff, *tables)


def restore_kernel(mine, columns, *refs):
    frames, length, width = columns.shape
    known = refs[:frames]
    feh, fel, ieh, iel, foh, fol, ioh, iol, out = refs[frames:]
    half = length // 2
    count = feh.shape[0] // 2
    for shift in range(frames):
        f = lax.rem(mine[0] + frames - shift, frames)
        low = columns[f, :half, :]
        high = columns[f, half:, :]
        limit = known[shift][length : length + 1, :]
        parts = []
        for first, field, tables in (
            (length // 8 + 2, low + high, (feh, fel, ieh, iel)),
            (length // 8 + 1, low - high, (foh, fol, ioh, iol)),
        ):
            spectrum = product(tables[0], tables[1], field)
            index = lax.broadcasted_iota(jnp.int32, spectrum.shape, 0)
            k = first + 2 * jnp.where(index < count, index, index - count)
            spectrum = jnp.where(k.astype(jnp.float32) > limit, spectrum, 0.0)
            parts.append(product(tables[2], tables[3], spectrum))
        out[f, :half, :] = known[shift][:half, :] + (parts[0] + parts[1])
        out[f, half:, :] = known[shift][half:length, :] + (parts[0] - parts[1])

    block = 32

    def smooth(i, carry):
        at = pl.ds(pl.multiple_of(i * block, block), block)
        anchor = [out[f, at, :] for f in range(frames)]
        current = anchor
        for _ in range(2):
            fluxes = []
            for f in range(frames - 1):
                d = current[f + 1] - current[f]
                fluxes.append(d * lax.rsqrt(d * d + 1.0))
            following = []
            for f in range(frames):
                flow = 0.0
                if f > 0:
                    flow = flow + fluxes[f - 1]
                if f < frames - 1:
                    flow = flow - fluxes[f]
                following.append(
                    current[f] - tv_step_size * ((current[f] - anchor[f]) + tv_weight * flow)
                )
            current = following
        for f in range(frames):
            out[f, at, :] = current[f]
        return carry

    lax.fori_loop(0, length // block, smooth, 0)


def restore(mine, columns, known, tables):
    whole = pl.BlockSpec(memory_space=pltpu.VMEM)
    return pl.pallas_call(
        restore_kernel,
        in_specs=[pl.BlockSpec(memory_space=pltpu.SMEM)] + [whole] * (1 + len(known) + len(tables)),
        out_specs=whole,
        out_shape=jax.ShapeDtypeStruct(columns.shape, jnp.float32),
        name="restore",
    )(mine, columns, *known, *tables)


def pack_kernel(field, out, sems):
    teams, slabs, _, width = out.shape
    copies = []
    for t in range(teams):
        for s in range(slabs):
            at = pl.ds((s * teams + t) * width, width)
            copies.append(
                pltpu.make_async_copy(field.at[:, at], out.at[t, s], sems.at[t * slabs + s])
            )
    for copy in copies:
        copy.start()
    for copy in copies:
        copy.wait()


def pack(field, teams, slabs):
    planes, pixels = field.shape
    width = pixels // (teams * slabs)
    if width % 128:
        return field.reshape(planes, slabs, teams, width).transpose(2, 1, 0, 3)
    return pl.pallas_call(
        pack_kernel,
        in_specs=[pl.BlockSpec(memory_space=pl.ANY)],
        out_specs=pl.BlockSpec(memory_space=pltpu.VMEM),
        out_shape=jax.ShapeDtypeStruct((teams, slabs, planes, width), jnp.float32),
        scratch_shapes=[pltpu.SemaphoreType.DMA((teams * slabs,))],
        name="pack",
    )(field)


def unpack_kernel(parts, out, sems):
    teams, slabs, _, width = parts.shape
    copies = []
    for t in range(teams):
        for s in range(slabs):
            at = pl.ds((s * teams + t) * width, width)
            copies.append(
                pltpu.make_async_copy(parts.at[t, s], out.at[:, at], sems.at[t * slabs + s])
            )
    for copy in copies:
        copy.start()
    for copy in copies:
        copy.wait()


def unpack(parts):
    teams, slabs, planes, width = parts.shape
    if width % 128:
        return parts.transpose(2, 1, 0, 3).reshape(planes, teams * slabs * width)
    return pl.pallas_call(
        unpack_kernel,
        in_specs=[pl.BlockSpec(memory_space=pltpu.VMEM)],
        out_specs=pl.BlockSpec(memory_space=pl.ANY),
        out_shape=jax.ShapeDtypeStruct((planes, teams * slabs * width), jnp.float32),
        scratch_shapes=[pltpu.SemaphoreType.DMA((teams * slabs,))],
        name="unpack",
    )(parts)


def on_device(volume, measured, cutoff):
    _, planes, pixels = volume.shape
    teams = lax.axis_size("frame")
    slabs = lax.axis_size("slab")
    mine = lax.axis_index("frame")
    length = planes * slabs
    width = pixels // (teams * slabs)
    axes = ("frame", "slab")

    sent = pack(volume[0], teams, slabs).reshape(teams * slabs, planes, width)
    columns = lax.all_to_all(sent, axes, split_axis=0, concat_axis=0, tiled=True)

    known = []
    own_tables = measured_tables(length)
    for shift in range(teams - 1, -1, -1):
        start = lax.rem(mine + shift, teams) * width
        part = measured_part(
            lax.dynamic_slice_in_dim(measured[0], start, width, axis=2),
            lax.dynamic_slice_in_dim(cutoff, start, width, axis=1),
            own_tables,
        )
        if shift:
            part = lax.ppermute(part, "frame", [(t, (t + shift) % teams) for t in range(teams)])
        known.insert(0, part)

    done = restore(
        mine.reshape(1), columns.reshape(teams, length, width), known, band_tables(length)
    )
    done = done.reshape(teams * slabs, planes, width)
    done = lax.all_to_all(done, axes, split_axis=0, concat_axis=0, tiled=True)
    return unpack(done.reshape(teams, slabs, planes, width))[None]


def solution(mesh):
    placed = (P("frame", "slab", None), P("frame", None, None, "slab"), P("frame", "slab"))
    return jax.shard_map(
        on_device, mesh=mesh, in_specs=placed, out_specs=P("frame", "slab", None), check_vma=False
    )
```

time: 308 us -> 129 us (0.42); the launches traced: 303 us -> 129 us
  matrix products: 91.2 us -> 0 us
  other arithmetic: 51.4 us -> 0 us
  Pallas kernels: 0 us -> 30 us
  local copies, waits for them, and re-layouts: 33.2 us -> 6.5 us
  waiting for transfers between devices: 52.6 us -> 30.9 us
  starting transfers between devices: 16 us -> 7.58 us
  blocking collectives: 58 us -> 54 us
    dot_general x4 -> x0, matrix products: 91.2 us -> none  [the longest x1 23.6 us: on_device(): jnp.dot(sin_table, imag_part, precision=highest, preferred_element_type=j...]
    unnamed x1 -> x0, other arithmetic: 38.4 us -> none
    pallas_call x0 -> x5, Pallas kernels: none -> 30 us  [the longest x2 14.3 us: measured_part(): pl.pallas_call(measured_kernel, grid=(columns // width,), in_specs=[pl.Bl...]
    unnamed x8 -> x6, local copies, waits for them, and re-layouts: 21.8 us -> 1.33 us
    all_to_all x1, waiting for transfers between devices: 43 us -> 30.9 us  [on_device(): lax.all_to_all(sent, axes, split_axis=0, concat_axis=0, tiled=True)]
    ppermute x4 -> x1, waiting for transfers between devices: 9.62 us -> 0.01 us  [on_device(): lax.ppermute(part, 'frame', [(t, (t + shift) % teams) for t in range(team...]
    all_to_all x4 -> x0, local copies, waits for them, and re-layouts: 9.28 us -> none  [the longest x2 5 us: on_device(): lax.all_to_all(volume, 'slab', split_axis=2, concat_axis=1, tiled=True)]
    all_to_all x1 -> x0, other arithmetic: 7.26 us -> none  [on_device(): lax.all_to_all(volume, 'slab', split_axis=2, concat_axis=1, tiled=True)]
  transfers between devices with their start and end apart: 5 -> 2, of which waited for: 5 -> 1; matrix products, arithmetic and copies ran while one was open for 0% -> 4% of each run, Pallas kernels for 0% -> 11%
where the time goes in v1:
time: 129 us
  blocking collectives  54 us (42%)
  waiting for transfers between devices  30.9 us (24%)
  Pallas kernels  30 us (23%)
  starting transfers between devices  7.58 us (6%)
  local copies, waits for them, and re-layouts  6.5 us (5%)
    all_to_all x1, blocking collectives, on_device(): done = lax.all_to_all(done, axes, split_axis=0, concat_axis=0, tiled=True)  54 us
    all_to_all x1, waiting for transfers between devices, on_device(): lax.all_to_all(sent, axes, split_axis=0, concat_axis=0, tiled=True)  30.9 us
    pallas_call x2, Pallas kernels, measured_part(): pl.pallas_call(measured_kernel, grid=(columns // width,), in_specs=[pl.Bl...  14.3 us
    pallas_call x1, Pallas kernels, restore(): pl.pallas_call(restore_kernel, in_specs=[pl.BlockSpec(memory_space=pltpu....  9.46 us
    all_to_all x1, starting transfers between devices, on_device(): lax.all_to_all(sent, axes, split_axis=0, concat_axis=0, tiled=True)  7.33 us
    dynamic_slice x1, local copies, waits for them, and re-layouts, on_device(): lax.dynamic_slice_in_dim(measured[0], start, width, axis=2)  4.57 us
    pallas_call x1, Pallas kernels, pack(): pl.pallas_call(pack_kernel, in_specs=[pl.BlockSpec(memory_space=pl.ANY)],...  3.16 us
    pallas_call x1, Pallas kernels, unpack(): pl.pallas_call(unpack_kernel, in_specs=[pl.BlockSpec(memory_space=pltpu.V...  3.16 us
  transfers between devices with their start and end apart: 2, of which 1 were waited for; matrix products, arithmetic and copies ran while one was open for 4% of the time, Pallas kernels for 11%

profile of v1, /device:TPU:0, one launch (start us, length us, event | category | flops | bytes accessed | tf_op | source)
XLA Modules:
  0.0 129.0 jit_solution(11465122219060222417)
XLA Ops:
  0.0 3.2 %pack.1 = f32[2,16,64,256]{3,2,1,0:T(8,128)} custom-call(f32[64,8192]{1,0:T(8,128)} %bitcast.15), custom_call_target="tpu_custom_call" | custom-call | tf_op jit(solution)/shard_map/pack/pallas_call | solution.py:181
  3.2 0.0 copy-start.2
  3.2 7.3 %all-to-all-start = ((f32[32,64,256]{2,1,0:T(8,128)}), f32[32,64,256]{2,1,0:T(8,128)S(1)}, u32[]{:S(2)}, u32[]{:S(2)}) async-start(f32[32,64,256]{2,1,0:T(8,128)} %bitcast.13), calls=%async_computation | async-start | bytes 4194304 | tf_op jit(solution)/shard_map/all_to_all | solution.py:230
  10.5 0.0 copy-done.2
  10.6 0.6 constant_dynamic-slice_fusion
  11.2 4.6 %dynamic-slice_bitcast_fusion = (f32[2,1024,256]{2,1,0:T(8,128)}, f32[2,1024,256]{2,1,0:T(8,128)}) fusion(f32[1,2,1024,512]{3,2,1,0:T(8,128)} %param.16, s32[]{:T(128)S(6)} %select_n.9, s32[]{:T(128)S(6)} %select_n.8), kind=kLoop, calls=%fused_computation | loop fusion | bytes 8388616 | tf_op jit(solution)/shard_map/dynamic_slice | solution.py:237
  15.7 7.1 %measured_part.3 = f32[1032,256]{1,0:T(8,128)} custom-call(f32[2,1024,256]{2,1,0:T(8,128)} %get-tuple-element.5.measured, s32[1,256]{1,0:T(1,128)} %get-tuple-element.7.cutoff, bf16[512,1024]{1,0:T(8,128)(2,1)} %constant.45.clone.even_high, bf16[512,1024]{1,0:T(8,128)(2,1)} %constant.46.clone.even_low, bf16[512,1024]{1,0:T(8,128)(2,1)} %constant.47.clone.odd_high, ...), custom_call_target="tpu_custom_call" | custom-call | tf_op jit(solution)/shard_map/measured_part/pallas_call | solution.py:83
  22.8 0.2 collective-permute-start
  23.1 7.1 %measured_part.2.refs_0_ = f32[1032,256]{1,0:T(8,128)} custom-call(f32[2,1024,256]{2,1,0:T(8,128)} %get-tuple-element.6.measured, s32[1,256]{1,0:T(1,128)} %get-tuple-element.8.cutoff, bf16[512,1024]{1,0:T(8,128)(2,1)} %constant.45.clone.even_high, bf16[512,1024]{1,0:T(8,128)(2,1)} %constant.46.clone.even_low, bf16[512,1024]{1,0:T(8,128)(2,1)} %constant.47.clone.odd_high, ...), custom_call_target="tpu_custom_call" | custom-call | tf_op jit(solution)/shard_map/measured_part/pallas_call | solution.py:83
  30.2 0.0 collective-permute-done.refs_1_
  30.2 0.0 copy-start.1
  30.2 30.9 %all-to-all-done = f32[32,64,256]{2,1,0:T(8,128)S(1)} async-done(((f32[32,64,256]{2,1,0:T(8,128)}), f32[32,64,256]{2,1,0:T(8,128)S(1)}, u32[]{:S(2)}, u32[]{:S(2)}) %all-to-all-start) | async-done | bytes 2097184 | tf_op jit(solution)/shard_map/all_to_all | solution.py:230
  61.1 0.0 copy-start
  61.1 0.0 copy-done.1
  61.1 1.3 %copy-done = f32[32,64,256]{2,1,0:T(8,128)} copy-done((f32[32,64,256]{2,1,0:T(8,128)}, f32[32,64,256]{2,1,0:T(8,128)S(1)}, u32[]{:S(2)}) %copy-start) | copy-done | bytes 2097176
  62.4 9.5 %restore.1 = f32[2,1024,256]{2,1,0:T(8,128)} custom-call(s32[1]{0:T(128)} %bitcast.mine, f32[2,1024,256]{2,1,0:T(8,128)} %bitcast.11, f32[1032,256]{1,0:T(8,128)} %measured_part.2.refs_0_, f32[1032,256]{1,0:T(8,128)} %copy-done.1, bf16[384,512]{1,0:T(8,128)(2,1)} %constant.49.clone.refs_2_, bf16[384,512]{1,0:T(8,128)(2,1)} %constant.50.clone.refs_3_, ...), custom_call_target="tpu_custom_call" | custom-call | tf_op jit(solution)/shard_map/restore/pallas_call | solution.py:152
  71.9 54.0 %all_to_all.10 = f32[32,64,256]{2,1,0:T(8,128)} all-to-all(f32[32,64,256]{2,1,0:T(8,128)} %bitcast.12), channel_id=1, replica_groups=mesh['frame'=2,'slab'=16] {'frame','slab'}, dimensions={0} | all-to-all | bytes 4194304 | tf_op jit(solution)/shard_map/all_to_all | solution.py:249
  125.9 3.2 %unpack.1 = f32[64,8192]{1,0:T(8,128)} custom-call(f32[2,16,64,256]{3,2,1,0:T(8,128)} %bitcast.14), custom_call_target="tpu_custom_call" | custom-call | tf_op jit(solution)/shard_map/unpack/pallas_call | solution.py:210
Async XLA Ops:
  3.2 7.4 %copy-start.2 = (s32[1,512]{1,0:T(1,128)S(1)}, s32[1,512]{1,0:T(1,128)}, u32[]{:S(2)}) copy-start(s32[1,512]{1,0:T(1,128)} %param.17) | copy-start | bytes 6148
  3.2 57.9 %all-to-all-start = ((f32[32,64,256]{2,1,0:T(8,128)}), f32[32,64,256]{2,1,0:T(8,128)S(1)}, u32[]{:S(2)}, u32[]{:S(2)}) async-start(f32[32,64,256]{2,1,0:T(8,128)} %bitcast.13), calls=%async_computation | async-start | bytes 4194304 | tf_op jit(solution)/shard_map/all_to_all | solution.py:230
  22.8 7.4 %collective-permute-start = (f32[1032,256]{1,0:T(8,128)}, f32[1032,256]{1,0:T(8,128)S(1)}, u32[]{:S(2)}, u32[]{:S(2)}) collective-permute-start(f32[1032,256]{1,0:T(8,128)} %measured_part.3), channel_id=1, source_target_pairs={{0,16},{16,0},{1,17},{17,1},{2,18},{18,2},{3,19},{19,3},{4,20},{20... | collective-permute-start | bytes 3170312 | tf_op jit(solution)/shard_map/ppermute | solution.py:242
  30.2 30.9 %copy-start.1 = (f32[1032,256]{1,0:T(8,128)}, f32[1032,256]{1,0:T(8,128)S(1)}, u32[]{:S(2)}) copy-start(f32[1032,256]{1,0:T(8,128)S(1)} %collective-permute-done.refs_1_) | copy-start | bytes 3170308
  61.1 1.3 %copy-start = (f32[32,64,256]{2,1,0:T(8,128)}, f32[32,64,256]{2,1,0:T(8,128)S(1)}, u32[]{:S(2)}) copy-start(f32[32,64,256]{2,1,0:T(8,128)S(1)} %all-to-all-done) | copy-start | bytes 6291460

commit v2 on v1

v2 whole, which is shorter than its diff:
```python
import functools
import math

import jax
import jax.numpy as jnp
import numpy as np
from jax import lax
from jax.experimental import pallas as pl
from jax.experimental.pallas import tpu as pltpu
from jax.sharding import PartitionSpec as P

tv_step_size = 0.25
tv_weight = 1.0
EXTRA = 8


def split(array):
    high = array.astype(jnp.bfloat16)
    low = (array - high.astype(jnp.float32)).astype(jnp.bfloat16)
    return high, low


def product(table_high, table_low, array):
    high, low = split(array)
    dot = functools.partial(jnp.dot, preferred_element_type=jnp.float32)
    return dot(table_high[...], high) + (dot(table_high[...], low) + dot(table_low[...], high))


def in_vmem(array):
    return pltpu.with_memory_space_constraint(array, pltpu.VMEM)


def in_hbm(array):
    return pltpu.with_memory_space_constraint(array, pltpu.HBM)


def as_pair(table):
    table = table.astype(np.float32)
    high = table.astype(jnp.bfloat16)
    low = (table - high.astype(np.float32)).astype(jnp.bfloat16)
    return [jnp.asarray(high), jnp.asarray(low)]


def rows(length, first, count):
    k = first + 2 * np.arange(count)
    z = np.arange(length // 2)
    angle = (k[:, None] * z[None, :] % length) * (2.0 * math.pi / length)
    table = np.concatenate([np.cos(angle), -np.sin(angle)], axis=0) / math.sqrt(length)
    return k, table


def band_tables(length):
    count = 3 * length // 16
    result = []
    for first in (length // 8 + 2, length // 8 + 1):
        k, table = rows(length, first, count)
        weight = np.where(k == length // 2, 1.0, 2.0)
        result += as_pair(table * np.concatenate([weight, weight])[:, None])
        result += as_pair(table.T)
    return result


def measured_tables(length):
    result = []
    for first in (0, 1):
        result += as_pair(rows(length, first, length // 2)[1].T)
    return result


def measured_kernel(measured, cutoff, even_high, even_low, odd_high, odd_low, out):
    length = measured.shape[1]
    half = length // 2
    limit = cutoff[...]
    parts = []
    for first, high, low in ((0, even_high, even_low), (1, odd_high, odd_low)):
        k = first + 2 * lax.broadcasted_iota(jnp.int32, (half, limit.shape[1]), 0)
        keep = jnp.where(k < half, k, length - k) <= limit
        stacked = [
            jnp.where(keep, measured[part, pl.ds(first, half, stride=2), :], 0.0) for part in (0, 1)
        ]
        parts.append(product(high, low, jnp.concatenate(stacked, axis=0)))
    out[:half, :] = parts[0] + parts[1]
    out[half:length, :] = parts[0] - parts[1]
    out[length:, :] = jnp.broadcast_to(limit.astype(jnp.float32), (EXTRA, limit.shape[1]))


def measured_part(measured, cutoff, tables):
    length, columns = measured.shape[1:]
    width = 128 if columns % 128 == 0 else columns
    whole = pl.BlockSpec(memory_space=pltpu.VMEM)
    return pl.pallas_call(
        measured_kernel,
        grid=(columns // width,),
        in_specs=[
            pl.BlockSpec((2, length, width), lambda i: (0, 0, i)),
            pl.BlockSpec((1, width), lambda i: (0, i)),
        ]
        + [whole] * len(tables),
        out_specs=pl.BlockSpec((length + EXTRA, width), lambda i: (0, i)),
        out_shape=jax.ShapeDtypeStruct((length + EXTRA, columns), jnp.float32),
        compiler_params=pltpu.CompilerParams(vmem_limit_bytes=32 * 1024 * 1024),
        name="measured_part",
    )(measured, cutoff, *[in_vmem(table) for table in tables])


def restore_kernel(mine, columns, *refs):
    slabs, frames, planes, width = columns.shape
    length = slabs * planes
    fetched = refs[frames + 2 : frames + 8]
    out = refs[frames + 8]
    known, sems = refs[-2:]
    tables = refs[frames : frames + 2] + refs[frames + 9 : -2]
    table_copies = [
        pltpu.make_async_copy(table, copy, sems.at[frames + i])
        for i, (table, copy) in enumerate(zip(fetched, tables[2:]))
    ]
    known_copies = [
        pltpu.make_async_copy(refs[shift], known.at[shift], sems.at[shift])
        for shift in range(frames)
    ]
    for copy in table_copies + known_copies:
        copy.start()
    half = length // 2
    count = tables[0].shape[0] // 2
    where = [lax.rem(mine[0] + frames - shift, frames) for shift in range(frames)]
    parts = []
    for side, first in ((0, length // 8 + 2), (1, length // 8 + 1)):
        index = lax.broadcasted_iota(jnp.int32, (2 * count, width), 0)
        k = (first + 2 * jnp.where(index < count, index, index - count)).astype(jnp.float32)
        if side == 1:
            for copy in table_copies[2:4]:
                copy.wait()
        spectra = []
        for f in where:
            low = columns[: slabs // 2, f].reshape(half, width)
            high = columns[slabs // 2 :, f].reshape(half, width)
            field = low + high if side == 0 else low - high
            spectra.append(product(tables[4 * side], tables[4 * side + 1], field))
        if side == 0:
            for copy in table_copies[:2] + known_copies:
                copy.wait()
        else:
            for copy in table_copies[4:]:
                copy.wait()
        for shift in range(frames):
            limit = known[shift, length : length + 1, :]
            spectrum = jnp.where(k > limit, spectra[shift], 0.0)
            parts.append(product(tables[4 * side + 2], tables[4 * side + 3], spectrum))
    for shift, f in enumerate(where):
        even, odd = parts[shift], parts[frames + shift]
        low = known[shift, :half, :] + (even + odd)
        high = known[shift, half:length, :] + (even - odd)
        out[: slabs // 2, f] = low.reshape(slabs // 2, planes, width)
        out[slabs // 2 :, f] = high.reshape(slabs // 2, planes, width)

    def smooth(i, carry):
        anchor = [out[i, f] for f in range(frames)]
        current = anchor
        for _ in range(2):
            fluxes = []
            for f in range(frames - 1):
                d = current[f + 1] - current[f]
                fluxes.append(d * lax.rsqrt(d * d + 1.0))
            following = []
            for f in range(frames):
                flow = 0.0
                if f > 0:
                    flow = flow + fluxes[f - 1]
                if f < frames - 1:
                    flow = flow - fluxes[f]
                following.append(
                    current[f] - tv_step_size * ((current[f] - anchor[f]) + tv_weight * flow)
                )
            current = following
        for f in range(frames):
            out[i, f] = current[f]
        return carry

    lax.fori_loop(0, slabs, smooth, 0)


def restore(mine, columns, known, tables):
    whole = pl.BlockSpec(memory_space=pltpu.VMEM)
    return pl.pallas_call(
        restore_kernel,
        in_specs=[pl.BlockSpec(memory_space=pltpu.SMEM), whole]
        + [pl.BlockSpec(memory_space=pltpu.HBM)] * len(known)
        + [whole] * 2
        + [pl.BlockSpec(memory_space=pltpu.HBM)] * (len(tables) - 2),
        out_specs=whole,
        out_shape=pltpu.VMEM(columns.shape, jnp.float32),
        scratch_shapes=[pltpu.VMEM(table.shape, table.dtype) for table in tables[2:]]
        + [
            pltpu.VMEM((len(known),) + known[0].shape, jnp.float32),
            pltpu.SemaphoreType.DMA((len(known) + len(tables),)),
        ],
        compiler_params=pltpu.CompilerParams(vmem_limit_bytes=24 * 1024 * 1024),
        name="restore",
    )(
        mine,
        in_vmem(columns),
        *map(in_hbm, known),
        *map(in_vmem, tables[:2]),
        *map(in_hbm, tables[2:]),
    )


def pack_kernel(field, out, rows, held, here, there):
    strips, strip, _ = rows.shape
    devices, _, width = out.shape
    at = [pl.ds(i * strip, strip) for i in range(strips)]
    loads = [
        pltpu.make_async_copy(field.at[at[i], :], rows.at[i], here.at[i]) for i in range(strips)
    ]
    stores = [
        pltpu.make_async_copy(held.at[i], out.at[:, at[i], :], there.at[i]) for i in range(strips)
    ]
    for load in loads:
        load.start()
    for i in range(strips):
        loads[i].wait()
        for d in range(devices):
            held[i, d] = rows[i, :, d * width : (d + 1) * width]
        stores[i].start()
    for store in stores:
        store.wait()


def pack(field, devices):
    planes, pixels = field.shape
    width = pixels // devices
    if width % 128:
        return field.reshape(planes, devices, width).transpose(1, 0, 2)
    strips = planes // 16
    return pl.pallas_call(
        pack_kernel,
        in_specs=[pl.BlockSpec(memory_space=pltpu.HBM)],
        out_specs=pl.BlockSpec(memory_space=pltpu.HBM),
        out_shape=pltpu.HBM((devices, planes, width), jnp.float32),
        scratch_shapes=[
            pltpu.VMEM((strips, 16, pixels), jnp.float32),
            pltpu.VMEM((strips, devices, 16, width), jnp.float32),
            pltpu.SemaphoreType.DMA((strips,)),
            pltpu.SemaphoreType.DMA((strips,)),
        ],
        compiler_params=pltpu.CompilerParams(vmem_limit_bytes=8 * 1024 * 1024),
        name="pack",
    )(in_hbm(field))


def unpack_kernel(parts, out, sems):
    devices, _, width = parts.shape
    copies = [
        pltpu.make_async_copy(parts.at[i], out.at[:, pl.ds(i * width, width)], sems.at[i])
        for i in range(devices)
    ]
    for copy in copies:
        copy.start()
    for copy in copies:
        copy.wait()


def unpack(parts):
    devices, planes, width = parts.shape
    if width % 128:
        return parts.transpose(1, 0, 2).reshape(planes, devices * width)
    return pl.pallas_call(
        unpack_kernel,
        in_specs=[pl.BlockSpec(memory_space=pltpu.VMEM)],
        out_specs=pl.BlockSpec(memory_space=pltpu.HBM),
        out_shape=jax.ShapeDtypeStruct((planes, devices * width), jnp.float32),
        scratch_shapes=[pltpu.SemaphoreType.DMA((devices,))],
        compiler_params=pltpu.CompilerParams(vmem_limit_bytes=4 * 1024 * 1024),
        name="unpack",
    )(in_vmem(parts))


def on_device(volume, measured, cutoff):
    _, planes, pixels = volume.shape
    teams = lax.axis_size("frame")
    slabs = lax.axis_size("slab")
    mine = lax.axis_index("frame")
    length = planes * slabs
    width = pixels // (teams * slabs)
    axes = ("slab", "frame")

    columns = pack(volume[0], teams * slabs)
    columns = lax.all_to_all(columns, axes, split_axis=0, concat_axis=0, tiled=True)

    known = []
    own_tables = measured_tables(length)
    for shift in range(teams - 1, -1, -1):
        start = lax.rem(mine + shift, teams) * width
        part = measured_part(
            lax.dynamic_slice_in_dim(measured[0], start, width, axis=2),
            lax.dynamic_slice_in_dim(cutoff, start, width, axis=1),
            own_tables,
        )
        if shift:
            part = lax.ppermute(part, "frame", [(t, (t + shift) % teams) for t in range(teams)])
        known.insert(0, part)

    columns = columns.reshape(slabs, teams, planes, width)
    done = restore(mine.reshape(1), columns, known, band_tables(length))
    done = done.reshape(teams * slabs, planes, width)
    done = lax.all_to_all(done, axes, split_axis=0, concat_axis=0, tiled=True)
    return unpack(done)[None]


def solution(mesh):
    placed = (P("frame", "slab", None), P("frame", None, None, "slab"), P("frame", "slab"))
    return jax.shard_map(
        on_device, mesh=mesh, in_specs=placed, out_specs=P("frame", "slab", None), check_vma=False
    )
```

time: 129 us -> 120 us (0.930)
  Pallas kernels: 30 us -> 19.2 us
  waiting for transfers between devices: 30.9 us -> 35.8 us
  local copies, waits for them, and re-layouts: 6.5 us -> 4.39 us
  blocking collectives: 54 us -> 52.6 us
    pallas_call x2, Pallas kernels: 14.3 us -> 8.14 us  [measured_part(): pl.pallas_call(measured_kernel, grid=(columns // width,), in_specs=[pl.Bl...]
    all_to_all x1, waiting for transfers between devices: 30.9 us -> 35.8 us  [on_device(): lax.all_to_all(columns, axes, split_axis=0, concat_axis=0, tiled=True)]
    pallas_call x1, Pallas kernels: 9.46 us -> 7.09 us  [restore(): pl.pallas_call(restore_kernel, in_specs=[pl.BlockSpec(memory_space=pltpu....]
    dynamic_slice x1, local copies, waits for them, and re-layouts: 4.57 us -> 2.66 us  [on_device(): lax.dynamic_slice_in_dim(measured[0], start, width, axis=2)]
    pallas_call x1, Pallas kernels: 3.16 us -> 1.57 us  [unpack(): pl.pallas_call(unpack_kernel, in_specs=[pl.BlockSpec(memory_space=pltpu.V...]
    all_to_all x1, blocking collectives: 54 us -> 52.6 us  [on_device(): done = lax.all_to_all(done, axes, split_axis=0, concat_axis=0, tiled=True)]
  transfers between devices with their start and end apart: 2 -> 2, of which waited for: 1 -> 1; matrix products, arithmetic and copies ran while one was open for 4% -> 2% of each run, Pallas kernels for 11% -> 7%
where the time goes in v2:
time: 120 us
  blocking collectives  52.6 us (44%)
  waiting for transfers between devices  35.8 us (30%)
  Pallas kernels  19.2 us (16%)
  starting transfers between devices  7.65 us (6%)
  local copies, waits for them, and re-layouts  4.39 us (4%)
    all_to_all x1, blocking collectives, on_device(): done = lax.all_to_all(done, axes, split_axis=0, concat_axis=0, tiled=True)  52.6 us
    all_to_all x1, waiting for transfers between devices, on_device(): lax.all_to_all(columns, axes, split_axis=0, concat_axis=0, tiled=True)  35.8 us
    pallas_call x2, Pallas kernels, measured_part(): pl.pallas_call(measured_kernel, grid=(columns // width,), in_specs=[pl.Bl...  8.14 us
    all_to_all x1, starting transfers between devices, on_device(): lax.all_to_all(columns, axes, split_axis=0, concat_axis=0, tiled=True)  7.33 us
    pallas_call x1, Pallas kernels, restore(): pl.pallas_call(restore_kernel, in_specs=[pl.BlockSpec(memory_space=pltpu....  7.09 us
    dynamic_slice x1, local copies, waits for them, and re-layouts, on_device(): lax.dynamic_slice_in_dim(measured[0], start, width, axis=2)  2.66 us
    pallas_call x1, Pallas kernels, pack(): pl.pallas_call(pack_kernel, in_specs=[pl.BlockSpec(memory_space=pltpu.HBM...  2.45 us
  transfers between devices with their start and end apart: 2, of which 1 were waited for; matrix products, arithmetic and copies ran while one was open for 2% of the time, Pallas kernels for 7%

profile of v2, /device:TPU:0, one launch (start us, length us, event | category | flops | bytes accessed | tf_op | source)
XLA Modules:
  0.0 119.8 jit_solution(5387475478872422492)
XLA Ops:
  0.0 2.5 %pack.1 = f32[32,64,256]{2,1,0:T(8,128)} custom-call(f32[64,8192]{1,0:T(8,128)} %bitcast.11), custom_call_target="tpu_custom_call" | custom-call | tf_op jit(solution)/shard_map/pack/pallas_call | solution.py:235
  2.5 0.0 copy-start.7
  2.5 7.3 %all-to-all-start = ((f32[32,64,256]{2,1,0:T(8,128)}), f32[32,64,256]{2,1,0:T(8,128)S(1)}, u32[]{:S(2)}, u32[]{:S(2)}) async-start(f32[32,64,256]{2,1,0:T(8,128)} %pack.1), calls=%async_computation | async-start | bytes 4194304 | tf_op jit(solution)/shard_map/all_to_all | solution.py:288
  9.8 0.0 copy-done.7
  9.9 0.0 copy-start.1
  9.9 0.0 copy-start.2
  9.9 0.0 copy-start.3
  9.9 0.0 copy-start.4
  9.9 2.7 %dynamic-slice_bitcast_fusion = (f32[2,1024,256]{2,1,0:T(8,128)S(1)}, f32[2,1024,256]{2,1,0:T(8,128)S(1)}) fusion(f32[1,2,1024,512]{3,2,1,0:T(8,128)} %param.16, s32[]{:T(128)S(6)} %select_n.9, s32[]{:T(128)S(6)} %select_n.8), kind=kLoop, calls=%fused_computation | loop fusion | bytes 8388616 | tf_op jit(solution)/shard_map/dynamic_slice | solution.py:295
  12.6 0.0 copy-done.1
  12.6 0.1 copy-done.2
  12.7 0.3 copy-done.3
  13.0 0.3 copy-done.4
  13.3 4.1 %measured_part.3 = f32[1032,256]{1,0:T(8,128)S(1)} custom-call(f32[2,1024,256]{2,1,0:T(8,128)S(1)} %get-tuple-element.5.measured, s32[1,256]{1,0:T(1,128)S(1)} %get-tuple-element.7.cutoff, bf16[512,1024]{1,0:T(8,128)(2,1)S(1)} %copy-done.1, bf16[512,1024]{1,0:T(8,128)(2,1)S(1)} %copy-done.2, bf16[512,1024]{1,0:T(8,128)(2,1)S(1)} %copy-done.3, ...), custom_call_target="tpu_custom_call" | custom-call | tf_op jit(solution)/shard_map/measured_part/pallas_call | solution.py:91
  17.4 0.3 collective-permute-start
  17.7 4.1 %measured_part.2.refs_0_ = f32[1032,256]{1,0:T(8,128)S(1)} custom-call(f32[2,1024,256]{2,1,0:T(8,128)S(1)} %get-tuple-element.6.measured, s32[1,256]{1,0:T(1,128)S(1)} %get-tuple-element.8.cutoff, bf16[512,1024]{1,0:T(8,128)(2,1)S(1)} %copy-done.1, bf16[512,1024]{1,0:T(8,128)(2,1)S(1)} %copy-done.2, bf16[512,1024]{1,0:T(8,128)(2,1)S(1)} %copy-done.3, ...), custom_call_target="tpu_custom_call" | custom-call | tf_op jit(solution)/shard_map/measured_part/pallas_call | solution.py:91
  21.8 0.0 copy-start
  21.8 1.0 copy-done
  22.8 0.0 collective-permute-done.refs_1_
  22.8 35.8 %all-to-all-done = f32[32,64,256]{2,1,0:T(8,128)S(1)} async-done(((f32[32,64,256]{2,1,0:T(8,128)}), f32[32,64,256]{2,1,0:T(8,128)S(1)}, u32[]{:S(2)}, u32[]{:S(2)}) %all-to-all-start) | async-done | bytes 2097184 | tf_op jit(solution)/shard_map/all_to_all | solution.py:288
  58.5 0.0 copy-done.6
  58.6 7.1 %restore.1 = f32[16,2,64,256]{3,2,1,0:T(8,128)S(1)} custom-call(s32[1]{0:T(128)} %bitcast.mine, f32[16,2,64,256]{3,2,1,0:T(8,128)S(1)} %bitcast.9, f32[1032,256]{1,0:T(8,128)} %copy-done, f32[1032,256]{1,0:T(8,128)} %collective-permute-done.refs_1_, bf16[384,512]{1,0:T(8,128)(2,1)S(1)} %copy-done.5, bf16[384,512]{1,0:T(8,128)(2,1)S(1)} %copy-done.6, ...), custom_call_target="tpu_custom_call" | custom-call | tf_op jit(solution)/shard_map/restore/pallas_call | solution.py:184
  65.6 52.6 %all_to_all.10.parts = f32[32,64,256]{2,1,0:T(8,128)S(1)} all-to-all(f32[32,64,256]{2,1,0:T(8,128)S(1)} %bitcast.10), channel_id=1, replica_groups=mesh['frame'=2,'slab'=16] {'slab','frame'}, dimensions={0} | all-to-all | bytes 4194304 | tf_op jit(solution)/shard_map/all_to_all | solution.py:306
  118.2 1.6 %unpack.1 = f32[64,8192]{1,0:T(8,128)} custom-call(f32[32,64,256]{2,1,0:T(8,128)S(1)} %all_to_all.10.parts), custom_call_target="tpu_custom_call" | custom-call | tf_op jit(solution)/shard_map/unpack/pallas_call | solution.py:267
  (4 shorter events, 0.0 us)
Async XLA Ops:
  2.5 7.4 %copy-start.7 = (s32[1,512]{1,0:T(1,128)S(1)}, s32[1,512]{1,0:T(1,128)}, u32[]{:S(2)}) copy-start(s32[1,512]{1,0:T(1,128)} %param.17) | copy-start | bytes 6148
  2.5 56.1 %all-to-all-start = ((f32[32,64,256]{2,1,0:T(8,128)}), f32[32,64,256]{2,1,0:T(8,128)S(1)}, u32[]{:S(2)}, u32[]{:S(2)}) async-start(f32[32,64,256]{2,1,0:T(8,128)} %pack.1), calls=%async_computation | async-start | bytes 4194304 | tf_op jit(solution)/shard_map/all_to_all | solution.py:288
  9.9 2.7 %copy-start.1 = (bf16[512,1024]{1,0:T(8,128)(2,1)S(1)}, bf16[512,1024]{1,0:T(8,128)(2,1)}, u32[]{:S(2)}) copy-start(bf16[512,1024]{1,0:T(8,128)(2,1)} %constant.45.clone.even_high) | copy-start | bytes 3145732
  9.9 2.8 %copy-start.2 = (bf16[512,1024]{1,0:T(8,128)(2,1)S(1)}, bf16[512,1024]{1,0:T(8,128)(2,1)}, u32[]{:S(2)}) copy-start(bf16[512,1024]{1,0:T(8,128)(2,1)} %constant.46.clone.even_low) | copy-start | bytes 3145732
  9.9 3.1 %copy-start.3 = (bf16[512,1024]{1,0:T(8,128)(2,1)S(1)}, bf16[512,1024]{1,0:T(8,128)(2,1)}, u32[]{:S(2)}) copy-start(bf16[512,1024]{1,0:T(8,128)(2,1)} %constant.47.clone.odd_high) | copy-start | bytes 3145732
  9.9 3.4 %copy-start.4 = (bf16[512,1024]{1,0:T(8,128)(2,1)S(1)}, bf16[512,1024]{1,0:T(8,128)(2,1)}, u32[]{:S(2)}) copy-start(bf16[512,1024]{1,0:T(8,128)(2,1)} %constant.48.clone.odd_low) | copy-start | bytes 3145732
  17.4 5.4 %collective-permute-start = (f32[1032,256]{1,0:T(8,128)S(1)}, f32[1032,256]{1,0:T(8,128)}, u32[]{:S(2)}, u32[]{:S(2)}) collective-permute-start(f32[1032,256]{1,0:T(8,128)S(1)} %measured_part.3), channel_id=1, source_target_pairs={{0,16},{16,0},{1,17},{17,1},{2,18},{18,2},{3,19},{19,3},{4,20},{20... | collective-permute-start | bytes 3170312 | tf_op jit(solution)/shard_map/ppermute | solution.py:300
  17.7 40.9 %copy-start.5 = (bf16[384,512]{1,0:T(8,128)(2,1)S(1)}, bf16[384,512]{1,0:T(8,128)(2,1)}, u32[]{:S(2)}) copy-start(bf16[384,512]{1,0:T(8,128)(2,1)} %constant.49.clone.refs_2_) | copy-start | bytes 1179652
  17.7 40.9 %copy-start.6 = (bf16[384,512]{1,0:T(8,128)(2,1)S(1)}, bf16[384,512]{1,0:T(8,128)(2,1)}, u32[]{:S(2)}) copy-start(bf16[384,512]{1,0:T(8,128)(2,1)} %constant.50.clone.refs_3_) | copy-start | bytes 1179652
  21.8 1.0 copy-start

commit v3 on v2

v3 whole, which is shorter than its diff:
```python
import functools
import math

import jax
import jax.numpy as jnp
import numpy as np
from jax import lax
from jax.experimental import pallas as pl
from jax.experimental.pallas import tpu as pltpu
from jax.sharding import PartitionSpec as P


tv_step_size = 0.25
tv_weight = 1.0
EXTRA = 8


def split(array):
    high = array.astype(jnp.bfloat16)
    low = (array - high.astype(jnp.float32)).astype(jnp.bfloat16)
    return high, low


def product(table_high, table_low, array):
    high, low = split(array)
    tables = [table_high[...], table_high[...], table_low[...]]
    return jnp.dot(
        jnp.concatenate(tables, axis=1),
        jnp.concatenate([high, low, high], axis=0),
        preferred_element_type=jnp.float32,
    )


def in_vmem(array):
    return pltpu.with_memory_space_constraint(array, pltpu.VMEM)


def in_hbm(array):
    return pltpu.with_memory_space_constraint(array, pltpu.HBM)


def as_pair(table):
    table = table.astype(np.float32)
    high = table.astype(jnp.bfloat16)
    low = (table - high.astype(np.float32)).astype(jnp.bfloat16)
    return [jnp.asarray(high), jnp.asarray(low)]


def rows(length, first, count):
    k = first + 2 * np.arange(count)
    z = np.arange(length // 2)
    angle = (k[:, None] * z[None, :] % length) * (2.0 * math.pi / length)
    table = np.concatenate([np.cos(angle), -np.sin(angle)], axis=0) / math.sqrt(length)
    return k, table


def band_tables(length):
    count = 3 * length // 16
    result = []
    for first in (length // 8 + 2, length // 8 + 1):
        k, table = rows(length, first, count)
        weight = np.where(k == length // 2, 1.0, 2.0)
        result += as_pair(table * np.concatenate([weight, weight])[:, None])
        result += as_pair(table.T)
    return result


def measured_tables(length):
    result = []
    for first in (0, 1):
        result += as_pair(rows(length, first, length // 2)[1].T)
    return result


def measured_kernel(measured, cutoff, even_high, even_low, odd_high, odd_low, out):
    length = measured.shape[1]
    half = length // 2
    limit = cutoff[...]
    parts = []
    for first, high, low in ((0, even_high, even_low), (1, odd_high, odd_low)):
        k = first + 2 * lax.broadcasted_iota(jnp.int32, (half, limit.shape[1]), 0)
        keep = jnp.where(k < half, k, length - k) <= limit
        stacked = [
            jnp.where(keep, measured[part, pl.ds(first, half, stride=2), :], 0.0) for part in (0, 1)
        ]
        parts.append(product(high, low, jnp.concatenate(stacked, axis=0)))
    out[:half, :] = parts[0] + parts[1]
    out[half:length, :] = parts[0] - parts[1]
    out[length:, :] = jnp.broadcast_to(limit.astype(jnp.float32), (EXTRA, limit.shape[1]))


def measured_part(measured, cutoff, tables, order, width):
    length = measured.shape[1]
    count = measured.shape[2] // width
    whole = pl.BlockSpec(memory_space=pltpu.VMEM)
    if width % 128:
        measured = measured.reshape(2, length, count, width).transpose(2, 0, 1, 3)
        field = pl.BlockSpec((None, 2, length, width), lambda i, order: (order[i], 0, 0, 0))
        cutoff = cutoff.reshape(count, 1, width)
        limit = pl.BlockSpec((None, 1, width), lambda i, order: (order[i], 0, 0))
    else:
        field = pl.BlockSpec((2, length, width), lambda i, order: (0, 0, order[i]))
        limit = pl.BlockSpec((1, width), lambda i, order: (0, order[i]))
    return pl.pallas_call(
        lambda order, *refs: measured_kernel(*refs),
        grid_spec=pltpu.PrefetchScalarGridSpec(
            num_scalar_prefetch=1,
            grid=(count,),
            in_specs=[field, limit] + [whole] * len(tables),
            out_specs=pl.BlockSpec((None, length + EXTRA, width), lambda i, order: (i, 0, 0)),
        ),
        out_shape=jax.ShapeDtypeStruct((count, length + EXTRA, width), jnp.float32),
        compiler_params=pltpu.CompilerParams(vmem_limit_bytes=32 * 1024 * 1024),
        name="measured_part",
    )(order, in_hbm(measured), cutoff, *map(in_hbm, tables))


def start_fetches(sources, targets, sems, first):
    copies = [
        pltpu.make_async_copy(source, target, sems.at[first + i])
        for i, (source, target) in enumerate(zip(sources, targets))
    ]
    for copy in copies:
        copy.start()
    return copies


def wait_all(copies):
    for copy in copies:
        copy.wait()


def kept_band(halves, limits, tables, table_copies, known_copies):
    half = halves[0][0].shape[0]
    count = tables[0].shape[0] // 2
    result = []
    for side, first in ((0, half // 4 + 2), (1, half // 4 + 1)):
        wait_all(table_copies[4 * side : 4 * side + 2])
        spectra = [
            product(
                tables[4 * side],
                tables[4 * side + 1],
                low + high if side == 0 else low - high,
            )
            for low, high in halves
        ]
        if side == 0:
            wait_all(known_copies)
        wait_all(table_copies[4 * side + 2 : 4 * side + 4])
        parts = []
        for spectrum, limit in zip(spectra, limits):
            index = lax.broadcasted_iota(jnp.int32, spectrum.shape, 0)
            k = (first + 2 * jnp.where(index < count, index, index - count)).astype(jnp.float32)
            spectrum = jnp.where(k > limit(), spectrum, 0.0)
            parts.append(product(tables[4 * side + 2], tables[4 * side + 3], spectrum))
        result.append(parts)
    return result


def restore_kernel(mine, columns, *refs):
    slabs, frames, planes, width = columns.shape
    length = slabs * planes
    half = length // 2
    known_refs, table_refs, result = refs[:frames], refs[frames : frames + 8], refs[frames + 8]
    tables, known, out, sems = refs[frames + 9 : frames + 17], refs[-3], refs[-2], refs[-1]
    stores = []
    table_copies = start_fetches(table_refs, tables, sems, frames)
    known_copies = start_fetches(known_refs, [known.at[f] for f in range(frames)], sems, 0)
    where = [lax.rem(mine[0] + frames - shift, frames) for shift in range(frames)]
    pair = frames == 2 and width == 128

    def lanes(pieces):
        return [jnp.concatenate(pieces, axis=1)] if pair else pieces

    low = lanes([columns[: slabs // 2, f].reshape(half, width) for f in where])
    high = lanes([columns[slabs // 2 :, f].reshape(half, width) for f in where])

    def limit(shift):
        return known[shift, length : length + 1, :]

    if pair:
        limits = [lambda: lanes([limit(0), limit(1)])[0]]
    else:
        limits = [functools.partial(limit, shift) for shift in range(frames)]
    parts = kept_band(list(zip(low, high)), limits, tables, table_copies, known_copies)
    if pair:
        parts = [[part[0][:, :width], part[0][:, width:]] for part in parts]
    for i in range(half // planes):
        at = slice(i * planes, (i + 1) * planes)
        for side in (0, 1):
            anchor = []
            for shift in range(frames):
                even, odd = parts[0][shift][at, :], parts[1][shift][at, :]
                here = slice(side * half + i * planes, side * half + (i + 1) * planes)
                anchor.append(known[shift, here, :] + (even + odd if side == 0 else even - odd))
            place = side * (slabs // 2) + i
            values = smooth_two(anchor) if frames == 2 else anchor
            for f, value in zip(where, values):
                out[place, f] = value
            if frames == 2:
                stores += start_fetches(
                    [out.at[place]], [result.at[place]], sems, frames + 8 + place
                )
    if frames == 2:
        wait_all(stores)
    else:

        def smooth(i, carry):
            for f, value in enumerate(smooth_all([out[i, f] for f in range(frames)])):
                out[i, f] = value
            return carry

        lax.fori_loop(0, slabs, smooth, 0)


def smooth_two(anchor):
    d = anchor[1] - anchor[0]
    first = d * lax.rsqrt(d * d + 1.0)
    d = d - (2.0 * tv_step_size * tv_weight) * first
    second = d * lax.rsqrt(d * d + 1.0)
    move = (tv_step_size * tv_weight) * ((1.0 - tv_step_size) * first + second)
    return anchor[0] + move, anchor[1] - move


def smooth_all(anchor):
    frames = len(anchor)
    current = anchor
    for _ in range(2):
        fluxes = []
        for f in range(frames - 1):
            d = current[f + 1] - current[f]
            fluxes.append(d * lax.rsqrt(d * d + 1.0))
        following = []
        for f in range(frames):
            flow = 0.0
            if f > 0:
                flow = flow + fluxes[f - 1]
            if f < frames - 1:
                flow = flow - fluxes[f]
            following.append(
                current[f] - tv_step_size * ((current[f] - anchor[f]) + tv_weight * flow)
            )
        current = following
    return current


def restore(mine, columns, known, tables):
    whole = pl.BlockSpec(memory_space=pltpu.VMEM)
    hbm = pl.BlockSpec(memory_space=pltpu.HBM)
    return pl.pallas_call(
        restore_kernel,
        in_specs=[pl.BlockSpec(memory_space=pltpu.SMEM), whole]
        + [hbm] * (len(known) + len(tables)),
        out_specs=hbm,
        out_shape=pltpu.HBM(columns.shape, jnp.float32),
        scratch_shapes=[pltpu.VMEM(table.shape, table.dtype) for table in tables]
        + [
            pltpu.VMEM((len(known),) + known[0].shape, jnp.float32),
            pltpu.VMEM(columns.shape, jnp.float32),
            pltpu.SemaphoreType.DMA((len(known) + len(tables) + columns.shape[0],)),
        ],
        compiler_params=pltpu.CompilerParams(vmem_limit_bytes=24 * 1024 * 1024),
        name="restore",
    )(mine, in_vmem(columns), *map(in_hbm, known), *map(in_hbm, tables))


def anchor_kernel(slab, *refs):
    pieces = len(refs) - 21
    piece_refs, known_ref, table_refs = refs[:pieces], refs[pieces], refs[pieces + 1 : pieces + 9]
    out, tables = refs[pieces + 9], refs[pieces + 10 : pieces + 18]
    columns, known, sems = refs[-3:]
    half = out.shape[0] // 2
    width = out.shape[1]
    piece_copies = start_fetches(
        piece_refs, [columns.at[slab[0] ^ d] for d in range(pieces)], sems, 9
    )
    table_copies = start_fetches(table_refs, tables, sems, 1)
    blocks, _, block = known_ref.shape
    first = blocks - width // block
    known_copies = start_fetches(
        [known_ref.at[b] for b in range(first, blocks)],
        [known.at[:, pl.ds((b - first) * block, block)] for b in range(first, blocks)],
        sems,
        9 + pieces,
    )
    wait_all(piece_copies)
    low = columns[: pieces // 2].reshape(half, width)
    high = columns[pieces // 2 :].reshape(half, width)
    (even,), (odd,) = kept_band(
        [(low, high)],
        [lambda: known[2 * half : 2 * half + 1, :]],
        tables,
        table_copies,
        known_copies,
    )
    out[:half, :] = known[:half, :] + (even + odd)
    out[half:, :] = known[half : 2 * half, :] + (even - odd)


def anchor_of(slab, pieces, known, tables):
    whole = pl.BlockSpec(memory_space=pltpu.VMEM)
    hbm = pl.BlockSpec(memory_space=pltpu.HBM)
    planes, width = pieces[0].shape
    return pl.pallas_call(
        anchor_kernel,
        in_specs=[pl.BlockSpec(memory_space=pltpu.SMEM)]
        + [whole] * len(pieces)
        + [hbm] * (1 + len(tables)),
        out_specs=whole,
        out_shape=jax.ShapeDtypeStruct((len(pieces) * planes, width), jnp.float32),
        scratch_shapes=[pltpu.VMEM(table.shape, table.dtype) for table in tables]
        + [
            pltpu.VMEM((len(pieces), planes, width), jnp.float32),
            pltpu.VMEM((known.shape[1], width), jnp.float32),
            pltpu.SemaphoreType.DMA((1 + len(tables) + len(pieces) + width // known.shape[2],)),
        ],
        compiler_params=pltpu.CompilerParams(vmem_limit_bytes=24 * 1024 * 1024),
        name="anchor",
    )(slab, *map(in_vmem, pieces), in_hbm(known), *map(in_hbm, tables))


def smooth_kernel(slab, own, other, *outs):
    planes = outs[0].shape[0]
    for d, out in enumerate(outs):
        at = pl.ds(pl.multiple_of((slab[0] ^ d) * planes, planes), planes)
        out[...] = smooth_two([own[at, :], other[at, :]])[0]


def smooth_pieces(slab, own, other, count):
    whole = pl.BlockSpec(memory_space=pltpu.VMEM)
    length, width = own.shape
    return pl.pallas_call(
        smooth_kernel,
        in_specs=[pl.BlockSpec(memory_space=pltpu.SMEM), whole, whole],
        out_specs=[whole] * count,
        out_shape=[jax.ShapeDtypeStruct((length // count, width), jnp.float32)] * count,
        compiler_params=pltpu.CompilerParams(vmem_limit_bytes=8 * 1024 * 1024),
        name="smooth",
    )(slab, own, other)


def pack_split_kernel(slab, field, *refs):
    outs = refs[:-6]
    rows, held, pieces, here, there, everywhere = refs[-6:]
    direct, piece_outs = outs[0], outs[1:]
    strips, strip, _ = rows.shape
    devices, _, width = direct.shape
    piece = pieces.shape[2]
    at = [pl.ds(i * strip, strip) for i in range(strips)]
    loads = start_fetches([field.at[a, :] for a in at], [rows.at[i] for i in range(strips)], here, 0)
    stores = []
    for i in range(strips):
        loads[i].wait()
        for d in range(devices):
            first = (d // 2) * 2 * piece + (d % 2) * width
            held[i, d] = rows[i, :, first : first + width]
        stores += start_fetches([held.at[i]], [direct.at[:, at[i], :]], there, i)
        for d in range(len(piece_outs)):
            first = pl.multiple_of((slab[0] ^ d) * (2 * piece) + piece, 128)
            pieces[d, i * strip : (i + 1) * strip, :] = rows[i, :, pl.ds(first, piece)]
    stores += start_fetches(
        [pieces.at[d] for d in range(len(piece_outs))], piece_outs, everywhere, 0
    )
    wait_all(stores)


def pack_split(slab, field, slabs):
    planes, pixels = field.shape
    piece = pixels // slabs // 2
    strips = planes // 16
    hbm = pl.BlockSpec(memory_space=pltpu.HBM)
    return pl.pallas_call(
        pack_split_kernel,
        in_specs=[pl.BlockSpec(memory_space=pltpu.SMEM), hbm],
        out_specs=[hbm] * (1 + slabs),
        out_shape=[pltpu.HBM((2 * slabs, planes, piece // 2), jnp.float32)]
        + [pltpu.HBM((planes, piece), jnp.float32)] * slabs,
        scratch_shapes=[
            pltpu.VMEM((strips, 16, pixels), jnp.float32),
            pltpu.VMEM((strips, 2 * slabs, 16, piece // 2), jnp.float32),
            pltpu.VMEM((slabs, planes, piece), jnp.float32),
            pltpu.SemaphoreType.DMA((strips,)),
            pltpu.SemaphoreType.DMA((strips,)),
            pltpu.SemaphoreType.DMA((slabs,)),
        ],
        compiler_params=pltpu.CompilerParams(vmem_limit_bytes=8 * 1024 * 1024),
        name="pack_split",
    )(slab, in_hbm(field))


def unpack_split_kernel(slab, direct, *refs):
    pieces, out, sems = refs[:-2], refs[-2], refs[-1]
    devices, _, width = direct.shape
    sources = [direct.at[d] for d in range(devices)] + list(pieces)
    piece = 2 * width
    targets = [
        out.at[:, pl.ds((d // 2) * 2 * piece + (d % 2) * width, width)] for d in range(devices)
    ]
    for d in range(len(pieces)):
        first = pl.multiple_of((slab[0] ^ d) * (2 * piece) + piece, 128)
        targets.append(out.at[:, pl.ds(first, piece)])
    wait_all(start_fetches(sources, targets, sems, 0))


def unpack_split(slab, direct, pieces):
    hbm = pl.BlockSpec(memory_space=pltpu.HBM)
    devices, planes, width = direct.shape
    return pl.pallas_call(
        unpack_split_kernel,
        in_specs=[pl.BlockSpec(memory_space=pltpu.SMEM)]
        + [pl.BlockSpec(memory_space=pltpu.VMEM)] * (1 + len(pieces)),
        out_specs=hbm,
        out_shape=jax.ShapeDtypeStruct((planes, 2 * devices * width), jnp.float32),
        scratch_shapes=[pltpu.SemaphoreType.DMA((devices + len(pieces),))],
        compiler_params=pltpu.CompilerParams(vmem_limit_bytes=4 * 1024 * 1024),
        name="unpack_split",
    )(slab, in_vmem(direct), *map(in_vmem, pieces))


def pack_kernel(field, out, rows, held, here, there):
    strips, strip, _ = rows.shape
    devices, _, width = out.shape
    at = [pl.ds(i * strip, strip) for i in range(strips)]
    loads = [
        pltpu.make_async_copy(field.at[at[i], :], rows.at[i], here.at[i]) for i in range(strips)
    ]
    stores = [
        pltpu.make_async_copy(held.at[i], out.at[:, at[i], :], there.at[i]) for i in range(strips)
    ]
    for load in loads:
        load.start()
    for i in range(strips):
        loads[i].wait()
        for d in range(devices):
            held[i, d] = rows[i, :, d * width : (d + 1) * width]
        stores[i].start()
    for store in stores:
        store.wait()


def pack(field, devices):
    planes, pixels = field.shape
    width = pixels // devices
    if width % 128:
        return field.reshape(planes, devices, width).transpose(1, 0, 2)
    strips = planes // 16
    return pl.pallas_call(
        pack_kernel,
        in_specs=[pl.BlockSpec(memory_space=pltpu.HBM)],
        out_specs=pl.BlockSpec(memory_space=pltpu.HBM),
        out_shape=pltpu.HBM((devices, planes, width), jnp.float32),
        scratch_shapes=[
            pltpu.VMEM((strips, 16, pixels), jnp.float32),
            pltpu.VMEM((strips, devices, 16, width), jnp.float32),
            pltpu.SemaphoreType.DMA((strips,)),
            pltpu.SemaphoreType.DMA((strips,)),
        ],
        compiler_params=pltpu.CompilerParams(vmem_limit_bytes=8 * 1024 * 1024),
        name="pack",
    )(in_hbm(field))


def unpack_kernel(parts, out, sems):
    devices, _, width = parts.shape
    copies = [
        pltpu.make_async_copy(parts.at[i], out.at[:, pl.ds(i * width, width)], sems.at[i])
        for i in range(devices)
    ]
    for copy in copies:
        copy.start()
    for copy in copies:
        copy.wait()


def unpack(parts):
    devices, planes, width = parts.shape
    if width % 128:
        return parts.transpose(1, 0, 2).reshape(planes, devices * width)
    return pl.pallas_call(
        unpack_kernel,
        in_specs=[pl.BlockSpec(memory_space=pltpu.VMEM)],
        out_specs=pl.BlockSpec(memory_space=pltpu.HBM),
        out_shape=jax.ShapeDtypeStruct((planes, devices * width), jnp.float32),
        scratch_shapes=[pltpu.SemaphoreType.DMA((devices,))],
        compiler_params=pltpu.CompilerParams(vmem_limit_bytes=4 * 1024 * 1024),
        name="unpack",
    )(in_vmem(parts))


def exchange(blocks):
    return lax.all_to_all(blocks, ("slab", "frame"), split_axis=0, concat_axis=0, tiled=True)


def known_parts(measured, cutoff, width):
    teams = lax.axis_size("frame")
    mine = lax.axis_index("frame")
    count = measured.shape[3] // width
    order = lax.rem(mine + jnp.arange(teams, dtype=jnp.int32), teams)
    order = jnp.concatenate([order, jnp.arange(teams, count, dtype=jnp.int32)])
    blocks = measured_part(measured[0], cutoff, measured_tables(measured.shape[2]), order, width)
    known = [blocks[0]]
    for shift in range(1, teams):
        pairs = [(t, (t + shift) % teams) for t in range(teams)]
        known.append(lax.ppermute(blocks[shift], "frame", pairs))
    return known, blocks


def on_device(volume, measured, cutoff):
    _, planes, pixels = volume.shape
    teams = lax.axis_size("frame")
    slabs = lax.axis_size("slab")
    mine = lax.axis_index("frame").reshape(1)
    length = planes * slabs
    if teams == 2 and slabs & (slabs - 1) == 0 and pixels % (512 * slabs) == 0:
        return split_on_device(volume, measured, cutoff)
    width = pixels // (teams * slabs)
    columns = exchange(pack(volume[0], teams * slabs))
    known, _ = known_parts(measured, cutoff, width)
    columns = columns.reshape(slabs, teams, planes, width)
    done = restore(mine, columns, known, band_tables(length))
    return unpack(exchange(done.reshape(teams * slabs, planes, width)))[None]


def permute(piece, distance):
    if distance == 0:
        return piece
    slabs = lax.axis_size("slab")
    return lax.ppermute(piece, "slab", [(s, s ^ distance) for s in range(slabs)])


def split_on_device(volume, measured, cutoff):
    _, planes, pixels = volume.shape
    slabs = lax.axis_size("slab")
    mine = lax.axis_index("frame").reshape(1)
    slab = lax.axis_index("slab").reshape(1)
    length = planes * slabs
    piece = pixels // slabs // 2
    width = piece // 2
    tables = band_tables(length)

    direct, *pieces = pack_split(slab, volume[0], slabs)
    columns = exchange(direct)
    order = sorted(range(slabs), key=lambda d: -d)
    arrived = [None] * slabs
    for d in order:
        arrived[d] = permute(pieces[d], d)

    known, blocks = known_parts(measured, cutoff, width)

    done = restore(mine, columns.reshape(slabs, 2, planes, width), known, tables)
    direct = exchange(done.reshape(2 * slabs, planes, width))

    anchor = anchor_of(slab, arrived, blocks, tables)
    other = lax.ppermute(anchor, "frame", [(0, 1), (1, 0)])
    pieces = smooth_pieces(slab, anchor, other, slabs)
    arrived = [None] * slabs
    for d in order:
        arrived[d] = permute(pieces[d], d)
    return unpack_split(slab, direct, arrived)[None]


def solution(mesh):
    placed = (P("frame", "slab", None), P("frame", None, None, "slab"), P("frame", "slab"))

    return jax.shard_map(
        on_device, mesh=mesh, in_specs=placed, out_specs=P("frame", "slab", None), check_vma=False
    )
```

time: 120 us -> 141 us (1.18)
  starting transfers between devices: 7.65 us -> 64.7 us
  blocking collectives: 52.6 us -> 0 us
  waiting for transfers between devices: 35.8 us -> 47 us
  Pallas kernels: 19.2 us -> 27.8 us
  local copies, waits for them, and re-layouts: 4.39 us -> 1.02 us
    ppermute x1 -> x32, starting transfers between devices: 0.32 us -> 53.8 us  [the longest x30 53.4 us: permute(): lax.ppermute(piece, 'slab', [(s, s ^ distance) for s in range(slabs)])]
    all_to_all x1 -> x0, blocking collectives: 52.6 us -> none  [on_device(): done = lax.all_to_all(done, axes, split_axis=0, concat_axis=0, tiled=True)]
    ppermute x1 -> x32, waiting for transfers between devices: 0.01 us -> 34.6 us  [the longest x30 30.1 us: permute(): lax.ppermute(piece, 'slab', [(s, s ^ distance) for s in range(slabs)])]
    all_to_all x1 -> x2, waiting for transfers between devices: 35.8 us -> 12.4 us  [exchange(): lax.all_to_all(blocks, ('slab', 'frame'), split_axis=0, concat_axis=0, ti...]
    pallas_call x4 -> x5, Pallas kernels: 12.2 us -> 22.1 us  [the longest x1 10.7 us: measured_part(): pl.pallas_call(lambda order, *refs: measured_kernel(*refs), grid_spec=plt...]
    all_to_all x1 -> x2, starting transfers between devices: 7.33 us -> 11 us  [exchange(): lax.all_to_all(blocks, ('slab', 'frame'), split_axis=0, concat_axis=0, ti...]
    dynamic_slice x2 -> x0, local copies, waits for them, and re-layouts: 2.67 us -> none  [the longest x1 2.66 us: on_device(): lax.dynamic_slice_in_dim(measured[0], start, width, axis=2)]
    unnamed x16 -> x34, local copies, waits for them, and re-layouts: 1.72 us -> 0.07 us
  transfers between devices with their start and end apart: 2 -> 34, of which waited for: 1 -> 15; matrix products, arithmetic and copies ran while one was open for 2% -> 1% of each run, Pallas kernels for 7% -> 12%
where the time goes in v3:
time: 141 us
  starting transfers between devices  64.7 us (46%)
  waiting for transfers between devices  47 us (33%)
  Pallas kernels  27.8 us (20%)
    ppermute x30, starting transfers between devices, permute(): lax.ppermute(piece, 'slab', [(s, s ^ distance) for s in range(slabs)])  53.4 us
    ppermute x30, waiting for transfers between devices, permute(): lax.ppermute(piece, 'slab', [(s, s ^ distance) for s in range(slabs)])  30.1 us
    all_to_all x2, waiting for transfers between devices, exchange(): lax.all_to_all(blocks, ('slab', 'frame'), split_axis=0, concat_axis=0, ti...  12.4 us
    all_to_all x2, starting transfers between devices, exchange(): lax.all_to_all(blocks, ('slab', 'frame'), split_axis=0, concat_axis=0, ti...  11 us
    pallas_call x1, Pallas kernels, measured_part(): pl.pallas_call(lambda order, *refs: measured_kernel(*refs), grid_spec=plt...  10.7 us
    pallas_call x1, Pallas kernels, anchor_of(): pl.pallas_call(anchor_kernel, in_specs=[pl.BlockSpec(memory_space=pltpu.S...  6.35 us
    pallas_call x1, Pallas kernels, restore(): pl.pallas_call(restore_kernel, in_specs=[pl.BlockSpec(memory_space=pltpu....  5.73 us
    pallas_call x1, Pallas kernels, pack_split(): pl.pallas_call(pack_split_kernel, in_specs=[pl.BlockSpec(memory_space=plt...  2.82 us
  transfers between devices with their start and end apart: 34, of which 15 were waited for; matrix products, arithmetic and copies ran while one was open for 1% of the time, Pallas kernels for 12%

profile of v3, /device:TPU:0, one launch (start us, length us, event | category | flops | bytes accessed | tf_op | source)
XLA Modules:
  0.0 140.8 jit_solution(13630905559527357344)
XLA Ops:
  0.0 2.8 %pack_split.1 = (f32[32,64,128]{2,1,0:T(8,128)}, f32[64,256]{1,0:T(8,128)}, f32[64,256]{1,0:T(8,128)}, f32[64,256]{1,0:T(8,128)}, f32[64,256]{1,0:T(8,128)}, /*i...) custom-call(s32[1]{0:T(128)} %bitcast.slab, ...), custom_call_target="tpu_custom_call" | custom-call | tf_op jit(solution)/shard_map/pack_split/pallas_call | solution.py:372
  2.8 7.3 %all-to-all-start = ((f32[32,64,128]{2,1,0:T(8,128)}), f32[32,64,128]{2,1,0:T(8,128)S(1)}, u32[]{:S(2)}, u32[]{:S(2)}) async-start(f32[32,64,128]{2,1,0:T(8,128)} %get-tuple-element.38), calls=%async_computation | async-start | bytes 2097152 | tf_op jit(solution)/shard_map/all_to_all | solution.py:491
  10.3 10.7 %measured_part.1.refs_16_ = f32[4,1032,128]{2,1,0:T(8,128)S(1)} custom-call(s32[4]{0:T(128)S(1)} %pad_add_fusion.order, f32[2,1024,512]{2,1,0:T(8,128)} %bitcast.13, s32[1,512]{1,0:T(1,128)S(1)} %copy-done.2, bf16[512,1024]{1,0:T(8,128)(2,1)} %constant.47.clone.refs_2_, bf16[512,1024]{1,0:T(8,128)(2,1)} %constant.48.clone.refs_3_, ...), custom_call_target="tpu_custom_call" | custom-call | tf_op jit(solution)/shard_map/measured_part/pallas_call | solution.py:104
  24.0 12.4 %all-to-all-done = f32[32,64,128]{2,1,0:T(8,128)S(1)} async-done(((f32[32,64,128]{2,1,0:T(8,128)}), f32[32,64,128]{2,1,0:T(8,128)S(1)}, u32[]{:S(2)}, u32[]{:S(2)}) %all-to-all-start) | async-done | bytes 1048608 | tf_op jit(solution)/shard_map/all_to_all | solution.py:491
  36.4 5.7 %restore.1 = f32[16,2,64,128]{3,2,1,0:T(8,128)} custom-call(s32[1]{0:T(128)} %bitcast.1.mine, f32[16,2,64,128]{3,2,1,0:T(8,128)S(1)} %bitcast.11, f32[1032,128]{1,0:T(8,128)} %get-tuple-element.72.refs_0_, f32[1032,128]{1,0:T(8,128)} %collective-permute-done.refs_1_, bf16[384,512]{1,0:T(8,128)(2,1)} %constant.39.clone.refs_2_.refs_17_, ...), custom_call_target="tpu_custom_call" | custom-call | tf_op jit(solution)/shard_map/restore/pallas_call | solution.py:250
  42.2 3.6 %all-to-all-start.1 = ((f32[32,64,128]{2,1,0:T(8,128)}), f32[32,64,128]{2,1,0:T(8,128)S(1)}, u32[]{:S(2)}, u32[]{:S(2)}) async-start(f32[32,64,128]{2,1,0:T(8,128)} %bitcast.12), calls=%async_computation.1 | async-start | bytes 2097152 | tf_op jit(solution)/shard_map/all_to_all | solution.py:491
  52.7 5.0 %collective-permute-done.1.refs_1_ = f32[64,256]{1,0:T(8,128)S(1)} collective-permute-done((f32[64,256]{1,0:T(8,128)}, f32[64,256]{1,0:T(8,128)S(1)}, u32[]{:S(2)}, u32[]{:S(2)}) %collective-permute-start.1) | collective-permute-done | bytes 65568 | tf_op jit(solution)/shard_map/ppermute | solution.py:528
  58.8 2.8 %collective-permute-start.7 = (f32[64,256]{1,0:T(8,128)S(1)}, f32[64,256]{1,0:T(8,128)S(1)}, u32[]{:S(2)}, u32[]{:S(2)}) collective-permute-start(f32[64,256]{1,0:T(8,128)S(1)} %copy-done.11), channel_id=1, source_target_pairs={{0,7},{1,6},{2,5},{3,4},{4,3},{5,2},{6,1},{7,0},{8,15},{9,14},{10,... | collective-permute-start | bytes 196616 | tf_op jit(solution)/shard_map/ppermute | solution.py:528
  65.2 5.6 %collective-permute-start.9 = (f32[64,256]{1,0:T(8,128)S(1)}, f32[64,256]{1,0:T(8,128)S(1)}, u32[]{:S(2)}, u32[]{:S(2)}) collective-permute-start(f32[64,256]{1,0:T(8,128)S(1)} %copy-done.9), channel_id=1, source_target_pairs={{0,9},{1,8},{2,11},{3,10},{4,13},{5,12},{6,15},{7,14},{8,1},{9,0},... | collective-permute-start | bytes 196616 | tf_op jit(solution)/shard_map/ppermute | solution.py:528
  70.9 2.3 %collective-permute-start.10 = (f32[64,256]{1,0:T(8,128)S(1)}, f32[64,256]{1,0:T(8,128)S(1)}, u32[]{:S(2)}, u32[]{:S(2)}) collective-permute-start(f32[64,256]{1,0:T(8,128)S(1)} %copy-done.8), channel_id=1, source_target_pairs={{0,10},{1,11},{2,8},{3,9},{4,14},{5,15},{6,12},{7,13},{8,2},{9,3},... | collective-permute-start | bytes 196616 | tf_op jit(solution)/shard_map/ppermute | solution.py:528
  75.4 5.7 %collective-permute-done.8.refs_8_ = f32[64,256]{1,0:T(8,128)S(1)} collective-permute-done((f32[64,256]{1,0:T(8,128)S(1)}, f32[64,256]{1,0:T(8,128)S(1)}, u32[]{:S(2)}, u32[]{:S(2)}) %collective-permute-start.8) | collective-permute-done | bytes 65568 | tf_op jit(solution)/shard_map/ppermute | solution.py:528
  81.1 2.2 %collective-permute-start.13 = (f32[64,256]{1,0:T(8,128)S(1)}, f32[64,256]{1,0:T(8,128)S(1)}, u32[]{:S(2)}, u32[]{:S(2)}) collective-permute-start(f32[64,256]{1,0:T(8,128)S(1)} %copy-done.5), channel_id=1, source_target_pairs={{0,13},{1,12},{2,15},{3,14},{4,9},{5,8},{6,11},{7,10},{8,5},{9,4},... | collective-permute-start | bytes 196616 | tf_op jit(solution)/shard_map/ppermute | solution.py:528
  83.4 3.4 %collective-permute-start.14 = (f32[64,256]{1,0:T(8,128)S(1)}, f32[64,256]{1,0:T(8,128)S(1)}, u32[]{:S(2)}, u32[]{:S(2)}) collective-permute-start(f32[64,256]{1,0:T(8,128)S(1)} %copy-done.4), channel_id=1, source_target_pairs={{0,14},{1,15},{2,12},{3,13},{4,10},{5,11},{6,8},{7,9},{8,6},{9,7},... | collective-permute-start | bytes 196616 | tf_op jit(solution)/shard_map/ppermute | solution.py:528
  90.6 4.2 %collective-permute-done.15.refs_15_ = f32[64,256]{1,0:T(8,128)S(1)} collective-permute-done((f32[64,256]{1,0:T(8,128)S(1)}, f32[64,256]{1,0:T(8,128)S(1)}, u32[]{:S(2)}, u32[]{:S(2)}) %collective-permute-start.15) | collective-permute-done | bytes 65568 | tf_op jit(solution)/shard_map/ppermute | solution.py:528
  94.7 6.4 %anchor.1.own = f32[1024,256]{1,0:T(8,128)S(1)} custom-call(s32[1]{0:T(128)} %bitcast.slab, f32[64,256]{1,0:T(8,128)S(1)} %copy-done.1, f32[64,256]{1,0:T(8,128)S(1)} %collective-permute-done.1.refs_1_, f32[64,256]{1,0:T(8,128)S(1)} %collective-permute-done.2.refs_2_, f32[64,256]{1,0:T(8,128)S(1)} %collective-permute-done.3.refs_3_, ...), custom_call_target="tpu_custom_call" | custom-call | tf_op jit(solution)/shard_map/anchor/pallas_call | solution.py:304
  101.2 2.6 %collective-permute-done.16.other = f32[1024,256]{1,0:T(8,128)S(1)} collective-permute-done((f32[1024,256]{1,0:T(8,128)S(1)}, f32[1024,256]{1,0:T(8,128)S(1)}, u32[]{:S(2)}, u32[]{:S(2)}) %collective-permute-start.16) | collective-permute-done | bytes 1048608 | tf_op jit(solution)/shard_map/ppermute | solution.py:554
  105.5 2.4 %collective-permute-start.19 = (f32[64,256]{1,0:T(8,128)S(1)}, f32[64,256]{1,0:T(8,128)S(1)}, u32[]{:S(2)}, u32[]{:S(2)}) collective-permute-start(f32[64,256]{1,0:T(8,128)S(1)} %get-tuple-element.58), channel_id=1, source_target_pairs={{0,3},{1,2},{2,1},{3,0},{4,7},{5,6},{6,5},{7,4},{8,11},{9,10},{10,... | collective-permute-start | bytes 196616 | tf_op jit(solution)/shard_map/ppermute | solution.py:528
  107.9 2.2 %collective-permute-start.20 = (f32[64,256]{1,0:T(8,128)S(1)}, f32[64,256]{1,0:T(8,128)S(1)}, u32[]{:S(2)}, u32[]{:S(2)}) collective-permute-start(f32[64,256]{1,0:T(8,128)S(1)} %get-tuple-element.59), channel_id=1, source_target_pairs={{0,4},{1,5},{2,6},{3,7},{4,0},{5,1},{6,2},{7,3},{8,12},{9,13},{10,... | collective-permute-start | bytes 196616 | tf_op jit(solution)/shard_map/ppermute | solution.py:528
  116.9 2.1 %collective-permute-start.26 = (f32[64,256]{1,0:T(8,128)S(1)}, f32[64,256]{1,0:T(8,128)S(1)}, u32[]{:S(2)}, u32[]{:S(2)}) collective-permute-start(f32[64,256]{1,0:T(8,128)S(1)} %get-tuple-element.65), channel_id=1, source_target_pairs={{0,10},{1,11},{2,8},{3,9},{4,14},{5,15},{6,12},{7,13},{8,2},{9,3},... | collective-permute-start | bytes 196616 | tf_op jit(solution)/shard_map/ppermute | solution.py:528
  119.0 2.7 %collective-permute-start.27 = (f32[64,256]{1,0:T(8,128)S(1)}, f32[64,256]{1,0:T(8,128)S(1)}, u32[]{:S(2)}, u32[]{:S(2)}) collective-permute-start(f32[64,256]{1,0:T(8,128)S(1)} %get-tuple-element.66), channel_id=1, source_target_pairs={{0,11},{1,10},{2,9},{3,8},{4,15},{5,14},{6,13},{7,12},{8,3},{9,2},... | collective-permute-start | bytes 196616 | tf_op jit(solution)/shard_map/ppermute | solution.py:528
  123.2 3.0 %collective-permute-done.24.refs_8_ = f32[64,256]{1,0:T(8,128)S(1)} collective-permute-done((f32[64,256]{1,0:T(8,128)S(1)}, f32[64,256]{1,0:T(8,128)S(1)}, u32[]{:S(2)}, u32[]{:S(2)}) %collective-permute-start.24) | collective-permute-done | bytes 65568 | tf_op jit(solution)/shard_map/ppermute | solution.py:528
  126.2 2.7 %collective-permute-done.25.refs_9_ = f32[64,256]{1,0:T(8,128)S(1)} collective-permute-done((f32[64,256]{1,0:T(8,128)S(1)}, f32[64,256]{1,0:T(8,128)S(1)}, u32[]{:S(2)}, u32[]{:S(2)}) %collective-permute-start.25) | collective-permute-done | bytes 65568 | tf_op jit(solution)/shard_map/ppermute | solution.py:528
  131.2 4.2 %collective-permute-start.31 = (f32[64,256]{1,0:T(8,128)S(1)}, f32[64,256]{1,0:T(8,128)S(1)}, u32[]{:S(2)}, u32[]{:S(2)}) collective-permute-start(f32[64,256]{1,0:T(8,128)S(1)} %get-tuple-element.70), channel_id=1, source_target_pairs={{0,15},{1,14},{2,13},{3,12},{4,11},{5,10},{6,9},{7,8},{8,7},{9,6},... | collective-permute-start | bytes 196616 | tf_op jit(solution)/shard_map/ppermute | solution.py:528
  136.0 3.1 %collective-permute-done.31.refs_15_ = f32[64,256]{1,0:T(8,128)S(1)} collective-permute-done((f32[64,256]{1,0:T(8,128)S(1)}, f32[64,256]{1,0:T(8,128)S(1)}, u32[]{:S(2)}, u32[]{:S(2)}) %collective-permute-start.31) | collective-permute-done | bytes 65568 | tf_op jit(solution)/shard_map/ppermute | solution.py:528
  (87 shorter events, 35.3 us)
Async XLA Ops:
  2.8 33.5 %all-to-all-start = ((f32[32,64,128]{2,1,0:T(8,128)}), f32[32,64,128]{2,1,0:T(8,128)S(1)}, u32[]{:S(2)}, u32[]{:S(2)}) async-start(f32[32,64,128]{2,1,0:T(8,128)} %get-tuple-element.38), calls=%async_computation | async-start | bytes 2097152 | tf_op jit(solution)/shard_map/all_to_all | solution.py:491
  42.2 96.9 %all-to-all-start.1 = ((f32[32,64,128]{2,1,0:T(8,128)}), f32[32,64,128]{2,1,0:T(8,128)S(1)}, u32[]{:S(2)}, u32[]{:S(2)}) async-start(f32[32,64,128]{2,1,0:T(8,128)} %bitcast.12), calls=%async_computation.1 | async-start | bytes 2097152 | tf_op jit(solution)/shard_map/all_to_all | solution.py:491
  45.9 11.8 %collective-permute-start.1 = (f32[64,256]{1,0:T(8,128)}, f32[64,256]{1,0:T(8,128)S(1)}, u32[]{:S(2)}, u32[]{:S(2)}) collective-permute-start(f32[64,256]{1,0:T(8,128)} %get-tuple-element.40), channel_id=1, source_target_pairs={{0,1},{1,0},{2,3},{3,2},{4,5},{5,4},{6,7},{7,6},{8,9},{9,8},{10,11... | collective-permute-start | bytes 196616 | tf_op jit(solution)/shard_map/ppermute | solution.py:528
  47.7 11.0 %collective-permute-start.2 = (f32[64,256]{1,0:T(8,128)S(1)}, f32[64,256]{1,0:T(8,128)S(1)}, u32[]{:S(2)}, u32[]{:S(2)}) collective-permute-start(f32[64,256]{1,0:T(8,128)S(1)} %copy-done.16), channel_id=1, source_target_pairs={{0,2},{1,3},{2,0},{3,1},{4,6},{5,7},{6,4},{7,5},{8,10},{9,11},{10,... | collective-permute-start | bytes 196616 | tf_op jit(solution)/shard_map/ppermute | solution.py:528
  49.2 12.4 %collective-permute-start.3 = (f32[64,256]{1,0:T(8,128)S(1)}, f32[64,256]{1,0:T(8,128)S(1)}, u32[]{:S(2)}, u32[]{:S(2)}) collective-permute-start(f32[64,256]{1,0:T(8,128)S(1)} %copy-done.15), channel_id=1, source_target_pairs={{0,3},{1,2},{2,1},{3,0},{4,7},{5,6},{6,5},{7,4},{8,11},{9,10},{10,... | collective-permute-start | bytes 196616 | tf_op jit(solution)/shard_map/ppermute | solution.py:528
  49.4 15.8 %collective-permute-start.4 = (f32[64,256]{1,0:T(8,128)S(1)}, f32[64,256]{1,0:T(8,128)S(1)}, u32[]{:S(2)}, u32[]{:S(2)}) collective-permute-start(f32[64,256]{1,0:T(8,128)S(1)} %copy-done.14), channel_id=1, source_target_pairs={{0,4},{1,5},{2,6},{3,7},{4,0},{5,1},{6,2},{7,3},{8,12},{9,13},{10,... | collective-permute-start | bytes 196616 | tf_op jit(solution)/shard_map/ppermute | solution.py:528
  51.2 19.7 %collective-permute-start.5 = (f32[64,256]{1,0:T(8,128)S(1)}, f32[64,256]{1,0:T(8,128)S(1)}, u32[]{:S(2)}, u32[]{:S(2)}) collective-permute-start(f32[64,256]{1,0:T(8,128)S(1)} %copy-done.13), channel_id=1, source_target_pairs={{0,5},{1,4},{2,7},{3,6},{4,1},{5,0},{6,3},{7,2},{8,13},{9,12},{10,... | collective-permute-start | bytes 196616 | tf_op jit(solution)/shard_map/ppermute | solution.py:528
  57.7 15.5 %collective-permute-start.6 = (f32[64,256]{1,0:T(8,128)S(1)}, f32[64,256]{1,0:T(8,128)S(1)}, u32[]{:S(2)}, u32[]{:S(2)}) collective-permute-start(f32[64,256]{1,0:T(8,128)S(1)} %copy-done.12), channel_id=1, source_target_pairs={{0,6},{1,7},{2,4},{3,5},{4,2},{5,3},{6,0},{7,1},{8,14},{9,15},{10,... | collective-permute-start | bytes 196616 | tf_op jit(solution)/shard_map/ppermute | solution.py:528
  58.8 15.9 %collective-permute-start.7 = (f32[64,256]{1,0:T(8,128)S(1)}, f32[64,256]{1,0:T(8,128)S(1)}, u32[]{:S(2)}, u32[]{:S(2)}) collective-permute-start(f32[64,256]{1,0:T(8,128)S(1)} %copy-done.11), channel_id=1, source_target_pairs={{0,7},{1,6},{2,5},{3,4},{4,3},{5,2},{6,1},{7,0},{8,15},{9,14},{10,... | collective-permute-start | bytes 196616 | tf_op jit(solution)/shard_map/ppermute | solution.py:528
  61.6 19.5 %collective-permute-start.8 = (f32[64,256]{1,0:T(8,128)S(1)}, f32[64,256]{1,0:T(8,128)S(1)}, u32[]{:S(2)}, u32[]{:S(2)}) collective-permute-start(f32[64,256]{1,0:T(8,128)S(1)} %copy-done.10), channel_id=1, source_target_pairs={{0,8},{1,9},{2,10},{3,11},{4,12},{5,13},{6,14},{7,15},{8,0},{9,1},... | collective-permute-start | bytes 196616 | tf_op jit(solution)/shard_map/ppermute | solution.py:528
  65.2 18.1 %collective-permute-start.9 = (f32[64,256]{1,0:T(8,128)S(1)}, f32[64,256]{1,0:T(8,128)S(1)}, u32[]{:S(2)}, u32[]{:S(2)}) collective-permute-start(f32[64,256]{1,0:T(8,128)S(1)} %copy-done.9), channel_id=1, source_target_pairs={{0,9},{1,8},{2,11},{3,10},{4,13},{5,12},{6,15},{7,14},{8,1},{9,0},... | collective-permute-start | bytes 196616 | tf_op jit(solution)/shard_map/ppermute | solution.py:528
  70.9 15.9 %collective-permute-start.10 = (f32[64,256]{1,0:T(8,128)S(1)}, f32[64,256]{1,0:T(8,128)S(1)}, u32[]{:S(2)}, u32[]{:S(2)}) collective-permute-start(f32[64,256]{1,0:T(8,128)S(1)} %copy-done.8), channel_id=1, source_target_pairs={{0,10},{1,11},{2,8},{3,9},{4,14},{5,15},{6,12},{7,13},{8,2},{9,3},... | collective-permute-start | bytes 196616 | tf_op jit(solution)/shard_map/ppermute | solution.py:528
  73.2 16.0 %collective-permute-start.11 = (f32[64,256]{1,0:T(8,128)S(1)}, f32[64,256]{1,0:T(8,128)S(1)}, u32[]{:S(2)}, u32[]{:S(2)}) collective-permute-start(f32[64,256]{1,0:T(8,128)S(1)} %copy-done.7), channel_id=1, source_target_pairs={{0,11},{1,10},{2,9},{3,8},{4,15},{5,14},{6,13},{7,12},{8,3},{9,2},... | collective-permute-start | bytes 196616 | tf_op jit(solution)/shard_map/ppermute | solution.py:528
  74.7 14.5 %collective-permute-start.12 = (f32[64,256]{1,0:T(8,128)S(1)}, f32[64,256]{1,0:T(8,128)S(1)}, u32[]{:S(2)}, u32[]{:S(2)}) collective-permute-start(f32[64,256]{1,0:T(8,128)S(1)} %copy-done.6), channel_id=1, source_target_pairs={{0,12},{1,13},{2,14},{3,15},{4,8},{5,9},{6,10},{7,11},{8,4},{9,5},... | collective-permute-start | bytes 196616 | tf_op jit(solution)/shard_map/ppermute | solution.py:528
  81.1 8.2 %collective-permute-start.13 = (f32[64,256]{1,0:T(8,128)S(1)}, f32[64,256]{1,0:T(8,128)S(1)}, u32[]{:S(2)}, u32[]{:S(2)}) collective-permute-start(f32[64,256]{1,0:T(8,128)S(1)} %copy-done.5), channel_id=1, source_target_pairs={{0,13},{1,12},{2,15},{3,14},{4,9},{5,8},{6,11},{7,10},{8,5},{9,4},... | collective-permute-start | bytes 196616 | tf_op jit(solution)/shard_map/ppermute | solution.py:528
  105.5 8.5 %collective-permute-start.19 = (f32[64,256]{1,0:T(8,128)S(1)}, f32[64,256]{1,0:T(8,128)S(1)}, u32[]{:S(2)}, u32[]{:S(2)}) collective-permute-start(f32[64,256]{1,0:T(8,128)S(1)} %get-tuple-element.58), channel_id=1, source_target_pairs={{0,3},{1,2},{2,1},{3,0},{4,7},{5,6},{6,5},{7,4},{8,11},{9,10},{10,... | collective-permute-start | bytes 196616 | tf_op jit(solution)/shard_map/ppermute | solution.py:528
  110.1 8.8 %collective-permute-start.22 = (f32[64,256]{1,0:T(8,128)S(1)}, f32[64,256]{1,0:T(8,128)S(1)}, u32[]{:S(2)}, u32[]{:S(2)}) collective-permute-start(f32[64,256]{1,0:T(8,128)S(1)} %get-tuple-element.61), channel_id=1, source_target_pairs={{0,6},{1,7},{2,4},{3,5},{4,2},{5,3},{6,0},{7,1},{8,14},{9,15},{10,... | collective-permute-start | bytes 196616 | tf_op jit(solution)/shard_map/ppermute | solution.py:528
  112.1 9.5 %collective-permute-start.23 = (f32[64,256]{1,0:T(8,128)S(1)}, f32[64,256]{1,0:T(8,128)S(1)}, u32[]{:S(2)}, u32[]{:S(2)}) collective-permute-start(f32[64,256]{1,0:T(8,128)S(1)} %get-tuple-element.62), channel_id=1, source_target_pairs={{0,7},{1,6},{2,5},{3,4},{4,3},{5,2},{6,1},{7,0},{8,15},{9,14},{10,... | collective-permute-start | bytes 196616 | tf_op jit(solution)/shard_map/ppermute | solution.py:528
  114.0 12.2 %collective-permute-start.24 = (f32[64,256]{1,0:T(8,128)S(1)}, f32[64,256]{1,0:T(8,128)S(1)}, u32[]{:S(2)}, u32[]{:S(2)}) collective-permute-start(f32[64,256]{1,0:T(8,128)S(1)} %get-tuple-element.63), channel_id=1, source_target_pairs={{0,8},{1,9},{2,10},{3,11},{4,12},{5,13},{6,14},{7,15},{8,0},{9,1},... | collective-permute-start | bytes 196616 | tf_op jit(solution)/shard_map/ppermute | solution.py:528
  116.0 12.9 %collective-permute-start.25 = (f32[64,256]{1,0:T(8,128)S(1)}, f32[64,256]{1,0:T(8,128)S(1)}, u32[]{:S(2)}, u32[]{:S(2)}) collective-permute-start(f32[64,256]{1,0:T(8,128)S(1)} %get-tuple-element.64), channel_id=1, source_target_pairs={{0,9},{1,8},{2,11},{3,10},{4,13},{5,12},{6,15},{7,14},{8,1},{9,0},... | collective-permute-start | bytes 196616 | tf_op jit(solution)/shard_map/ppermute | solution.py:528
  116.9 14.3 %collective-permute-start.26 = (f32[64,256]{1,0:T(8,128)S(1)}, f32[64,256]{1,0:T(8,128)S(1)}, u32[]{:S(2)}, u32[]{:S(2)}) collective-permute-start(f32[64,256]{1,0:T(8,128)S(1)} %get-tuple-element.65), channel_id=1, source_target_pairs={{0,10},{1,11},{2,8},{3,9},{4,14},{5,15},{6,12},{7,13},{8,2},{9,3},... | collective-permute-start | bytes 196616 | tf_op jit(solution)/shard_map/ppermute | solution.py:528
  119.0 16.4 %collective-permute-start.27 = (f32[64,256]{1,0:T(8,128)S(1)}, f32[64,256]{1,0:T(8,128)S(1)}, u32[]{:S(2)}, u32[]{:S(2)}) collective-permute-start(f32[64,256]{1,0:T(8,128)S(1)} %get-tuple-element.66), channel_id=1, source_target_pairs={{0,11},{1,10},{2,9},{3,8},{4,15},{5,14},{6,13},{7,12},{8,3},{9,2},... | collective-permute-start | bytes 196616 | tf_op jit(solution)/shard_map/ppermute | solution.py:528
  121.6 13.7 %collective-permute-start.28 = (f32[64,256]{1,0:T(8,128)S(1)}, f32[64,256]{1,0:T(8,128)S(1)}, u32[]{:S(2)}, u32[]{:S(2)}) collective-permute-start(f32[64,256]{1,0:T(8,128)S(1)} %get-tuple-element.67), channel_id=1, source_target_pairs={{0,12},{1,13},{2,14},{3,15},{4,8},{5,9},{6,10},{7,11},{8,4},{9,5},... | collective-permute-start | bytes 196616 | tf_op jit(solution)/shard_map/ppermute | solution.py:528
  126.2 9.1 %collective-permute-start.29 = (f32[64,256]{1,0:T(8,128)S(1)}, f32[64,256]{1,0:T(8,128)S(1)}, u32[]{:S(2)}, u32[]{:S(2)}) collective-permute-start(f32[64,256]{1,0:T(8,128)S(1)} %get-tuple-element.68), channel_id=1, source_target_pairs={{0,13},{1,12},{2,15},{3,14},{4,9},{5,8},{6,11},{7,10},{8,5},{9,4},... | collective-permute-start | bytes 196616 | tf_op jit(solution)/shard_map/ppermute | solution.py:528
  (27 other events, 501.8 us)

commit v4 on v3

--- a/solution.py
+++ b/solution.py
@@ -66,9 +66,13 @@
 
 
 def measured_tables(length):
+    count = 3 * length // 16
     result = []
     for first in (0, 1):
-        result += as_pair(rows(length, first, length // 2)[1].T)
+        low = rows(length, first, count)[1]
+        high = rows(length, 5 * length // 8 + first, count)[1]
+        parts = [low[:count], high[:count], low[count:], high[count:]]
+        result += as_pair(np.concatenate(parts, axis=0).T)
     return result
 
 
@@ -76,13 +80,22 @@
     length = measured.shape[1]
     half = length // 2
     limit = cutoff[...]
+    count = 3 * length // 16
+    edge = 3 * length // 8
     parts = []
     for first, high, low in ((0, even_high, even_low), (1, odd_high, odd_low)):
-        k = first + 2 * lax.broadcasted_iota(jnp.int32, (half, limit.shape[1]), 0)
-        keep = jnp.where(k < half, k, length - k) <= limit
-        stacked = [
-            jnp.where(keep, measured[part, pl.ds(first, half, stride=2), :], 0.0) for part in (0, 1)
-        ]
+        row = lax.broadcasted_iota(jnp.int32, (count, limit.shape[1]), 0)
+        k = first + 2 * row
+        stacked = []
+        for part in (0, 1):
+            below = measured[part, pl.ds(first, count, stride=2), :]
+            above = measured[part, pl.ds(length - edge + first, count, stride=2), :]
+            above = jnp.where(edge - k <= limit, above, 0.0)
+            if first == 0:
+                last = jnp.where(edge <= limit, measured[part, edge : edge + 1, :], 0.0)
+                joined = above + last if part == 0 else above - last
+                above = jnp.where(row == 0, joined, above)
+            stacked += [jnp.where(k <= limit, below, 0.0), above]
         parts.append(product(high, low, jnp.concatenate(stacked, axis=0)))
     out[:half, :] = parts[0] + parts[1]
     out[half:length, :] = parts[0] - parts[1]
@@ -162,9 +175,11 @@
     length = slabs * planes
     half = length // 2
     known_refs, table_refs, result = refs[:frames], refs[frames : frames + 8], refs[frames + 8]
-    tables, known, out, sems = refs[frames + 9 : frames + 17], refs[-3], refs[-2], refs[-1]
+    known, out, sems = refs[-3:]
+    fetched = refs[frames + 9 : -3]
+    tables = fetched
     stores = []
-    table_copies = start_fetches(table_refs, tables, sems, frames)
+    table_copies = start_fetches(table_refs, fetched, sems, frames)
     known_copies = start_fetches(known_refs, [known.at[f] for f in range(frames)], sems, 0)
     where = [lax.rem(mine[0] + frames - shift, frames) for shift in range(frames)]
     pair = frames == 2 and width == 128
@@ -250,7 +265,8 @@
     return pl.pallas_call(
         restore_kernel,
         in_specs=[pl.BlockSpec(memory_space=pltpu.SMEM), whole]
-        + [hbm] * (len(known) + len(tables)),
+        + [hbm] * len(known)
+        + [hbm] * len(tables),
         out_specs=hbm,
         out_shape=pltpu.HBM(columns.shape, jnp.float32),
         scratch_shapes=[pltpu.VMEM(table.shape, table.dtype) for table in tables]
@@ -267,14 +283,15 @@
 def anchor_kernel(slab, *refs):
     pieces = len(refs) - 21
     piece_refs, known_ref, table_refs = refs[:pieces], refs[pieces], refs[pieces + 1 : pieces + 9]
-    out, tables = refs[pieces + 9], refs[pieces + 10 : pieces + 18]
+    out, fetched = refs[pieces + 9], refs[pieces + 10 : -3]
+    tables = fetched
     columns, known, sems = refs[-3:]
     half = out.shape[0] // 2
     width = out.shape[1]
     piece_copies = start_fetches(
         piece_refs, [columns.at[slab[0] ^ d] for d in range(pieces)], sems, 9
     )
-    table_copies = start_fetches(table_refs, tables, sems, 1)
+    table_copies = start_fetches(table_refs, fetched, sems, 1)
     blocks, _, block = known_ref.shape
     first = blocks - width // block
     known_copies = start_fetches(
@@ -305,7 +322,8 @@
         anchor_kernel,
         in_specs=[pl.BlockSpec(memory_space=pltpu.SMEM)]
         + [whole] * len(pieces)
-        + [hbm] * (1 + len(tables)),
+        + [hbm]
+        + [hbm] * len(tables),
         out_specs=whole,
         out_shape=jax.ShapeDtypeStruct((len(pieces) * planes, width), jnp.float32),
         scratch_shapes=[pltpu.VMEM(table.shape, table.dtype) for table in tables]

time: 141 us -> 141 us (level)
  Pallas kernels: 27.8 us -> 25.8 us
  waiting for transfers between devices: 47 us -> 49 us
    all_to_all x2, waiting for transfers between devices: 12.4 us -> 14.4 us  [exchange(): lax.all_to_all(blocks, ('slab', 'frame'), split_axis=0, concat_axis=0, ti...]
    pallas_call x1, Pallas kernels: 10.7 us -> 8.64 us  [measured_part(): pl.pallas_call(lambda order, *refs: measured_kernel(*refs), grid_spec=plt...]
  transfers between devices with their start and end apart: 34 -> 34, of which waited for: 15 -> 15; matrix products, arithmetic and copies ran while one was open for 1% -> 1% of each run, Pallas kernels for 12% -> 11%
where the time goes in v4:
time: 141 us
  starting transfers between devices  64.7 us (46%)
  waiting for transfers between devices  49 us (35%)
  Pallas kernels  25.8 us (18%)
    ppermute x30, starting transfers between devices, permute(): lax.ppermute(piece, 'slab', [(s, s ^ distance) for s in range(slabs)])  53.4 us
    ppermute x30, waiting for transfers between devices, permute(): lax.ppermute(piece, 'slab', [(s, s ^ distance) for s in range(slabs)])  30.1 us
    all_to_all x2, waiting for transfers between devices, exchange(): lax.all_to_all(blocks, ('slab', 'frame'), split_axis=0, concat_axis=0, ti...  14.4 us
    all_to_all x2, starting transfers between devices, exchange(): lax.all_to_all(blocks, ('slab', 'frame'), split_axis=0, concat_axis=0, ti...  11 us
    pallas_call x1, Pallas kernels, measured_part(): pl.pallas_call(lambda order, *refs: measured_kernel(*refs), grid_spec=plt...  8.64 us
    pallas_call x1, Pallas kernels, anchor_of(): pl.pallas_call(anchor_kernel, in_specs=[pl.BlockSpec(memory_space=pltpu.S...  6.36 us
    pallas_call x1, Pallas kernels, restore(): pl.pallas_call(restore_kernel, in_specs=[pl.BlockSpec(memory_space=pltpu....  5.74 us
    pallas_call x1, Pallas kernels, pack_split(): pl.pallas_call(pack_split_kernel, in_specs=[pl.BlockSpec(memory_space=plt...  2.82 us
  transfers between devices with their start and end apart: 34, of which 15 were waited for; matrix products, arithmetic and copies ran while one was open for 1% of the time, Pallas kernels for 11%

profile of v4, /device:TPU:0, one launch (start us, length us, event | category | flops | bytes accessed | tf_op | source)
XLA Modules:
  0.0 140.8 jit_solution(4137354057227834159)
XLA Ops:
  0.0 2.8 %pack_split.1 = (f32[32,64,128]{2,1,0:T(8,128)}, f32[64,256]{1,0:T(8,128)}, f32[64,256]{1,0:T(8,128)}, f32[64,256]{1,0:T(8,128)}, f32[64,256]{1,0:T(8,128)}, /*i...) custom-call(s32[1]{0:T(128)} %bitcast.slab, ...), custom_call_target="tpu_custom_call" | custom-call | tf_op jit(solution)/shard_map/pack_split/pallas_call | solution.py:390
  2.8 7.3 %all-to-all-start = ((f32[32,64,128]{2,1,0:T(8,128)}), f32[32,64,128]{2,1,0:T(8,128)S(1)}, u32[]{:S(2)}, u32[]{:S(2)}) async-start(f32[32,64,128]{2,1,0:T(8,128)} %get-tuple-element.38), calls=%async_computation | async-start | bytes 2097152 | tf_op jit(solution)/shard_map/all_to_all | solution.py:509
  10.3 8.6 %measured_part.1.refs_16_ = f32[4,1032,128]{2,1,0:T(8,128)S(1)} custom-call(s32[4]{0:T(128)S(1)} %pad_add_fusion.order, f32[2,1024,512]{2,1,0:T(8,128)} %bitcast.13, s32[1,512]{1,0:T(1,128)S(1)} %copy-done.2, bf16[512,768]{1,0:T(8,128)(2,1)} %constant.47.clone.refs_2_, bf16[512,768]{1,0:T(8,128)(2,1)} %constant.48.clone.refs_3_, ...), custom_call_target="tpu_custom_call" | custom-call | tf_op jit(solution)/shard_map/measured_part/pallas_call | solution.py:117
  21.9 14.4 %all-to-all-done = f32[32,64,128]{2,1,0:T(8,128)S(1)} async-done(((f32[32,64,128]{2,1,0:T(8,128)}), f32[32,64,128]{2,1,0:T(8,128)S(1)}, u32[]{:S(2)}, u32[]{:S(2)}) %all-to-all-start) | async-done | bytes 1048608 | tf_op jit(solution)/shard_map/all_to_all | solution.py:509
  36.4 5.7 %restore.1 = f32[16,2,64,128]{3,2,1,0:T(8,128)} custom-call(s32[1]{0:T(128)} %bitcast.1.mine, f32[16,2,64,128]{3,2,1,0:T(8,128)S(1)} %bitcast.11, f32[1032,128]{1,0:T(8,128)} %get-tuple-element.72.refs_0_, f32[1032,128]{1,0:T(8,128)} %collective-permute-done.refs_1_, bf16[384,512]{1,0:T(8,128)(2,1)} %constant.39.clone.refs_2_.refs_17_, ...), custom_call_target="tpu_custom_call" | custom-call | tf_op jit(solution)/shard_map/restore/pallas_call | solution.py:265
  42.3 3.6 %all-to-all-start.1 = ((f32[32,64,128]{2,1,0:T(8,128)}), f32[32,64,128]{2,1,0:T(8,128)S(1)}, u32[]{:S(2)}, u32[]{:S(2)}) async-start(f32[32,64,128]{2,1,0:T(8,128)} %bitcast.12), calls=%async_computation.1 | async-start | bytes 2097152 | tf_op jit(solution)/shard_map/all_to_all | solution.py:509
  52.7 5.0 %collective-permute-done.1.refs_1_ = f32[64,256]{1,0:T(8,128)S(1)} collective-permute-done((f32[64,256]{1,0:T(8,128)}, f32[64,256]{1,0:T(8,128)S(1)}, u32[]{:S(2)}, u32[]{:S(2)}) %collective-permute-start.1) | collective-permute-done | bytes 65568 | tf_op jit(solution)/shard_map/ppermute | solution.py:546
  58.8 2.8 %collective-permute-start.7 = (f32[64,256]{1,0:T(8,128)S(1)}, f32[64,256]{1,0:T(8,128)S(1)}, u32[]{:S(2)}, u32[]{:S(2)}) collective-permute-start(f32[64,256]{1,0:T(8,128)S(1)} %copy-done.11), channel_id=1, source_target_pairs={{0,7},{1,6},{2,5},{3,4},{4,3},{5,2},{6,1},{7,0},{8,15},{9,14},{10,... | collective-permute-start | bytes 196616 | tf_op jit(solution)/shard_map/ppermute | solution.py:546
  65.2 5.6 %collective-permute-start.9 = (f32[64,256]{1,0:T(8,128)S(1)}, f32[64,256]{1,0:T(8,128)S(1)}, u32[]{:S(2)}, u32[]{:S(2)}) collective-permute-start(f32[64,256]{1,0:T(8,128)S(1)} %copy-done.9), channel_id=1, source_target_pairs={{0,9},{1,8},{2,11},{3,10},{4,13},{5,12},{6,15},{7,14},{8,1},{9,0},... | collective-permute-start | bytes 196616 | tf_op jit(solution)/shard_map/ppermute | solution.py:546
  70.9 2.3 %collective-permute-start.10 = (f32[64,256]{1,0:T(8,128)S(1)}, f32[64,256]{1,0:T(8,128)S(1)}, u32[]{:S(2)}, u32[]{:S(2)}) collective-permute-start(f32[64,256]{1,0:T(8,128)S(1)} %copy-done.8), channel_id=1, source_target_pairs={{0,10},{1,11},{2,8},{3,9},{4,14},{5,15},{6,12},{7,13},{8,2},{9,3},... | collective-permute-start | bytes 196616 | tf_op jit(solution)/shard_map/ppermute | solution.py:546
  75.4 5.7 %collective-permute-done.8.refs_8_ = f32[64,256]{1,0:T(8,128)S(1)} collective-permute-done((f32[64,256]{1,0:T(8,128)S(1)}, f32[64,256]{1,0:T(8,128)S(1)}, u32[]{:S(2)}, u32[]{:S(2)}) %collective-permute-start.8) | collective-permute-done | bytes 65568 | tf_op jit(solution)/shard_map/ppermute | solution.py:546
  81.1 2.2 %collective-permute-start.13 = (f32[64,256]{1,0:T(8,128)S(1)}, f32[64,256]{1,0:T(8,128)S(1)}, u32[]{:S(2)}, u32[]{:S(2)}) collective-permute-start(f32[64,256]{1,0:T(8,128)S(1)} %copy-done.5), channel_id=1, source_target_pairs={{0,13},{1,12},{2,15},{3,14},{4,9},{5,8},{6,11},{7,10},{8,5},{9,4},... | collective-permute-start | bytes 196616 | tf_op jit(solution)/shard_map/ppermute | solution.py:546
  83.4 3.4 %collective-permute-start.14 = (f32[64,256]{1,0:T(8,128)S(1)}, f32[64,256]{1,0:T(8,128)S(1)}, u32[]{:S(2)}, u32[]{:S(2)}) collective-permute-start(f32[64,256]{1,0:T(8,128)S(1)} %copy-done.4), channel_id=1, source_target_pairs={{0,14},{1,15},{2,12},{3,13},{4,10},{5,11},{6,8},{7,9},{8,6},{9,7},... | collective-permute-start | bytes 196616 | tf_op jit(solution)/shard_map/ppermute | solution.py:546
  90.6 4.2 %collective-permute-done.15.refs_15_ = f32[64,256]{1,0:T(8,128)S(1)} collective-permute-done((f32[64,256]{1,0:T(8,128)S(1)}, f32[64,256]{1,0:T(8,128)S(1)}, u32[]{:S(2)}, u32[]{:S(2)}) %collective-permute-start.15) | collective-permute-done | bytes 65568 | tf_op jit(solution)/shard_map/ppermute | solution.py:546
  94.7 6.4 %anchor.1.own = f32[1024,256]{1,0:T(8,128)S(1)} custom-call(s32[1]{0:T(128)} %bitcast.slab, f32[64,256]{1,0:T(8,128)S(1)} %copy-done.1, f32[64,256]{1,0:T(8,128)S(1)} %collective-permute-done.1.refs_1_, f32[64,256]{1,0:T(8,128)S(1)} %collective-permute-done.2.refs_2_, f32[64,256]{1,0:T(8,128)S(1)} %collective-permute-done.3.refs_3_, ...), custom_call_target="tpu_custom_call" | custom-call | tf_op jit(solution)/shard_map/anchor/pallas_call | solution.py:321
  101.2 2.6 %collective-permute-done.16.other = f32[1024,256]{1,0:T(8,128)S(1)} collective-permute-done((f32[1024,256]{1,0:T(8,128)S(1)}, f32[1024,256]{1,0:T(8,128)S(1)}, u32[]{:S(2)}, u32[]{:S(2)}) %collective-permute-start.16) | collective-permute-done | bytes 1048608 | tf_op jit(solution)/shard_map/ppermute | solution.py:572
  105.5 2.4 %collective-permute-start.19 = (f32[64,256]{1,0:T(8,128)S(1)}, f32[64,256]{1,0:T(8,128)S(1)}, u32[]{:S(2)}, u32[]{:S(2)}) collective-permute-start(f32[64,256]{1,0:T(8,128)S(1)} %get-tuple-element.58), channel_id=1, source_target_pairs={{0,3},{1,2},{2,1},{3,0},{4,7},{5,6},{6,5},{7,4},{8,11},{9,10},{10,... | collective-permute-start | bytes 196616 | tf_op jit(solution)/shard_map/ppermute | solution.py:546
  107.9 2.2 %collective-permute-start.20 = (f32[64,256]{1,0:T(8,128)S(1)}, f32[64,256]{1,0:T(8,128)S(1)}, u32[]{:S(2)}, u32[]{:S(2)}) collective-permute-start(f32[64,256]{1,0:T(8,128)S(1)} %get-tuple-element.59), channel_id=1, source_target_pairs={{0,4},{1,5},{2,6},{3,7},{4,0},{5,1},{6,2},{7,3},{8,12},{9,13},{10,... | collective-permute-start | bytes 196616 | tf_op jit(solution)/shard_map/ppermute | solution.py:546
  116.9 2.1 %collective-permute-start.26 = (f32[64,256]{1,0:T(8,128)S(1)}, f32[64,256]{1,0:T(8,128)S(1)}, u32[]{:S(2)}, u32[]{:S(2)}) collective-permute-start(f32[64,256]{1,0:T(8,128)S(1)} %get-tuple-element.65), channel_id=1, source_target_pairs={{0,10},{1,11},{2,8},{3,9},{4,14},{5,15},{6,12},{7,13},{8,2},{9,3},... | collective-permute-start | bytes 196616 | tf_op jit(solution)/shard_map/ppermute | solution.py:546
  119.0 2.7 %collective-permute-start.27 = (f32[64,256]{1,0:T(8,128)S(1)}, f32[64,256]{1,0:T(8,128)S(1)}, u32[]{:S(2)}, u32[]{:S(2)}) collective-permute-start(f32[64,256]{1,0:T(8,128)S(1)} %get-tuple-element.66), channel_id=1, source_target_pairs={{0,11},{1,10},{2,9},{3,8},{4,15},{5,14},{6,13},{7,12},{8,3},{9,2},... | collective-permute-start | bytes 196616 | tf_op jit(solution)/shard_map/ppermute | solution.py:546
  123.2 3.0 %collective-permute-done.24.refs_8_ = f32[64,256]{1,0:T(8,128)S(1)} collective-permute-done((f32[64,256]{1,0:T(8,128)S(1)}, f32[64,256]{1,0:T(8,128)S(1)}, u32[]{:S(2)}, u32[]{:S(2)}) %collective-permute-start.24) | collective-permute-done | bytes 65568 | tf_op jit(solution)/shard_map/ppermute | solution.py:546
  126.2 2.7 %collective-permute-done.25.refs_9_ = f32[64,256]{1,0:T(8,128)S(1)} collective-permute-done((f32[64,256]{1,0:T(8,128)S(1)}, f32[64,256]{1,0:T(8,128)S(1)}, u32[]{:S(2)}, u32[]{:S(2)}) %collective-permute-start.25) | collective-permute-done | bytes 65568 | tf_op jit(solution)/shard_map/ppermute | solution.py:546
  131.2 4.2 %collective-permute-start.31 = (f32[64,256]{1,0:T(8,128)S(1)}, f32[64,256]{1,0:T(8,128)S(1)}, u32[]{:S(2)}, u32[]{:S(2)}) collective-permute-start(f32[64,256]{1,0:T(8,128)S(1)} %get-tuple-element.70), channel_id=1, source_target_pairs={{0,15},{1,14},{2,13},{3,12},{4,11},{5,10},{6,9},{7,8},{8,7},{9,6},... | collective-permute-start | bytes 196616 | tf_op jit(solution)/shard_map/ppermute | solution.py:546
  136.0 3.1 %collective-permute-done.31.refs_15_ = f32[64,256]{1,0:T(8,128)S(1)} collective-permute-done((f32[64,256]{1,0:T(8,128)S(1)}, f32[64,256]{1,0:T(8,128)S(1)}, u32[]{:S(2)}, u32[]{:S(2)}) %collective-permute-start.31) | collective-permute-done | bytes 65568 | tf_op jit(solution)/shard_map/ppermute | solution.py:546
  (87 shorter events, 35.3 us)
Async XLA Ops:
  2.8 33.5 %all-to-all-start = ((f32[32,64,128]{2,1,0:T(8,128)}), f32[32,64,128]{2,1,0:T(8,128)S(1)}, u32[]{:S(2)}, u32[]{:S(2)}) async-start(f32[32,64,128]{2,1,0:T(8,128)} %get-tuple-element.38), calls=%async_computation | async-start | bytes 2097152 | tf_op jit(solution)/shard_map/all_to_all | solution.py:509
  42.3 96.9 %all-to-all-start.1 = ((f32[32,64,128]{2,1,0:T(8,128)}), f32[32,64,128]{2,1,0:T(8,128)S(1)}, u32[]{:S(2)}, u32[]{:S(2)}) async-start(f32[32,64,128]{2,1,0:T(8,128)} %bitcast.12), calls=%async_computation.1 | async-start | bytes 2097152 | tf_op jit(solution)/shard_map/all_to_all | solution.py:509
  45.9 11.8 %collective-permute-start.1 = (f32[64,256]{1,0:T(8,128)}, f32[64,256]{1,0:T(8,128)S(1)}, u32[]{:S(2)}, u32[]{:S(2)}) collective-permute-start(f32[64,256]{1,0:T(8,128)} %get-tuple-element.40), channel_id=1, source_target_pairs={{0,1},{1,0},{2,3},{3,2},{4,5},{5,4},{6,7},{7,6},{8,9},{9,8},{10,11... | collective-permute-start | bytes 196616 | tf_op jit(solution)/shard_map/ppermute | solution.py:546
  47.7 11.0 %collective-permute-start.2 = (f32[64,256]{1,0:T(8,128)S(1)}, f32[64,256]{1,0:T(8,128)S(1)}, u32[]{:S(2)}, u32[]{:S(2)}) collective-permute-start(f32[64,256]{1,0:T(8,128)S(1)} %copy-done.16), channel_id=1, source_target_pairs={{0,2},{1,3},{2,0},{3,1},{4,6},{5,7},{6,4},{7,5},{8,10},{9,11},{10,... | collective-permute-start | bytes 196616 | tf_op jit(solution)/shard_map/ppermute | solution.py:546
  49.2 12.4 %collective-permute-start.3 = (f32[64,256]{1,0:T(8,128)S(1)}, f32[64,256]{1,0:T(8,128)S(1)}, u32[]{:S(2)}, u32[]{:S(2)}) collective-permute-start(f32[64,256]{1,0:T(8,128)S(1)} %copy-done.15), channel_id=1, source_target_pairs={{0,3},{1,2},{2,1},{3,0},{4,7},{5,6},{6,5},{7,4},{8,11},{9,10},{10,... | collective-permute-start | bytes 196616 | tf_op jit(solution)/shard_map/ppermute | solution.py:546
  49.5 15.8 %collective-permute-start.4 = (f32[64,256]{1,0:T(8,128)S(1)}, f32[64,256]{1,0:T(8,128)S(1)}, u32[]{:S(2)}, u32[]{:S(2)}) collective-permute-start(f32[64,256]{1,0:T(8,128)S(1)} %copy-done.14), channel_id=1, source_target_pairs={{0,4},{1,5},{2,6},{3,7},{4,0},{5,1},{6,2},{7,3},{8,12},{9,13},{10,... | collective-permute-start | bytes 196616 | tf_op jit(solution)/shard_map/ppermute | solution.py:546
  51.2 19.7 %collective-permute-start.5 = (f32[64,256]{1,0:T(8,128)S(1)}, f32[64,256]{1,0:T(8,128)S(1)}, u32[]{:S(2)}, u32[]{:S(2)}) collective-permute-start(f32[64,256]{1,0:T(8,128)S(1)} %copy-done.13), channel_id=1, source_target_pairs={{0,5},{1,4},{2,7},{3,6},{4,1},{5,0},{6,3},{7,2},{8,13},{9,12},{10,... | collective-permute-start | bytes 196616 | tf_op jit(solution)/shard_map/ppermute | solution.py:546
  57.7 15.5 %collective-permute-start.6 = (f32[64,256]{1,0:T(8,128)S(1)}, f32[64,256]{1,0:T(8,128)S(1)}, u32[]{:S(2)}, u32[]{:S(2)}) collective-permute-start(f32[64,256]{1,0:T(8,128)S(1)} %copy-done.12), channel_id=1, source_target_pairs={{0,6},{1,7},{2,4},{3,5},{4,2},{5,3},{6,0},{7,1},{8,14},{9,15},{10,... | collective-permute-start | bytes 196616 | tf_op jit(solution)/shard_map/ppermute | solution.py:546
  58.8 15.9 %collective-permute-start.7 = (f32[64,256]{1,0:T(8,128)S(1)}, f32[64,256]{1,0:T(8,128)S(1)}, u32[]{:S(2)}, u32[]{:S(2)}) collective-permute-start(f32[64,256]{1,0:T(8,128)S(1)} %copy-done.11), channel_id=1, source_target_pairs={{0,7},{1,6},{2,5},{3,4},{4,3},{5,2},{6,1},{7,0},{8,15},{9,14},{10,... | collective-permute-start | bytes 196616 | tf_op jit(solution)/shard_map/ppermute | solution.py:546
  61.6 19.5 %collective-permute-start.8 = (f32[64,256]{1,0:T(8,128)S(1)}, f32[64,256]{1,0:T(8,128)S(1)}, u32[]{:S(2)}, u32[]{:S(2)}) collective-permute-start(f32[64,256]{1,0:T(8,128)S(1)} %copy-done.10), channel_id=1, source_target_pairs={{0,8},{1,9},{2,10},{3,11},{4,12},{5,13},{6,14},{7,15},{8,0},{9,1},... | collective-permute-start | bytes 196616 | tf_op jit(solution)/shard_map/ppermute | solution.py:546
  65.2 18.1 %collective-permute-start.9 = (f32[64,256]{1,0:T(8,128)S(1)}, f32[64,256]{1,0:T(8,128)S(1)}, u32[]{:S(2)}, u32[]{:S(2)}) collective-permute-start(f32[64,256]{1,0:T(8,128)S(1)} %copy-done.9), channel_id=1, source_target_pairs={{0,9},{1,8},{2,11},{3,10},{4,13},{5,12},{6,15},{7,14},{8,1},{9,0},... | collective-permute-start | bytes 196616 | tf_op jit(solution)/shard_map/ppermute | solution.py:546
  70.9 15.9 %collective-permute-start.10 = (f32[64,256]{1,0:T(8,128)S(1)}, f32[64,256]{1,0:T(8,128)S(1)}, u32[]{:S(2)}, u32[]{:S(2)}) collective-permute-start(f32[64,256]{1,0:T(8,128)S(1)} %copy-done.8), channel_id=1, source_target_pairs={{0,10},{1,11},{2,8},{3,9},{4,14},{5,15},{6,12},{7,13},{8,2},{9,3},... | collective-permute-start | bytes 196616 | tf_op jit(solution)/shard_map/ppermute | solution.py:546
  73.2 16.0 %collective-permute-start.11 = (f32[64,256]{1,0:T(8,128)S(1)}, f32[64,256]{1,0:T(8,128)S(1)}, u32[]{:S(2)}, u32[]{:S(2)}) collective-permute-start(f32[64,256]{1,0:T(8,128)S(1)} %copy-done.7), channel_id=1, source_target_pairs={{0,11},{1,10},{2,9},{3,8},{4,15},{5,14},{6,13},{7,12},{8,3},{9,2},... | collective-permute-start | bytes 196616 | tf_op jit(solution)/shard_map/ppermute | solution.py:546
  74.7 14.5 %collective-permute-start.12 = (f32[64,256]{1,0:T(8,128)S(1)}, f32[64,256]{1,0:T(8,128)S(1)}, u32[]{:S(2)}, u32[]{:S(2)}) collective-permute-start(f32[64,256]{1,0:T(8,128)S(1)} %copy-done.6), channel_id=1, source_target_pairs={{0,12},{1,13},{2,14},{3,15},{4,8},{5,9},{6,10},{7,11},{8,4},{9,5},... | collective-permute-start | bytes 196616 | tf_op jit(solution)/shard_map/ppermute | solution.py:546
  81.1 8.2 %collective-permute-start.13 = (f32[64,256]{1,0:T(8,128)S(1)}, f32[64,256]{1,0:T(8,128)S(1)}, u32[]{:S(2)}, u32[]{:S(2)}) collective-permute-start(f32[64,256]{1,0:T(8,128)S(1)} %copy-done.5), channel_id=1, source_target_pairs={{0,13},{1,12},{2,15},{3,14},{4,9},{5,8},{6,11},{7,10},{8,5},{9,4},... | collective-permute-start | bytes 196616 | tf_op jit(solution)/shard_map/ppermute | solution.py:546
  105.5 8.5 %collective-permute-start.19 = (f32[64,256]{1,0:T(8,128)S(1)}, f32[64,256]{1,0:T(8,128)S(1)}, u32[]{:S(2)}, u32[]{:S(2)}) collective-permute-start(f32[64,256]{1,0:T(8,128)S(1)} %get-tuple-element.58), channel_id=1, source_target_pairs={{0,3},{1,2},{2,1},{3,0},{4,7},{5,6},{6,5},{7,4},{8,11},{9,10},{10,... | collective-permute-start | bytes 196616 | tf_op jit(solution)/shard_map/ppermute | solution.py:546
  110.1 8.8 %collective-permute-start.22 = (f32[64,256]{1,0:T(8,128)S(1)}, f32[64,256]{1,0:T(8,128)S(1)}, u32[]{:S(2)}, u32[]{:S(2)}) collective-permute-start(f32[64,256]{1,0:T(8,128)S(1)} %get-tuple-element.61), channel_id=1, source_target_pairs={{0,6},{1,7},{2,4},{3,5},{4,2},{5,3},{6,0},{7,1},{8,14},{9,15},{10,... | collective-permute-start | bytes 196616 | tf_op jit(solution)/shard_map/ppermute | solution.py:546
  112.1 9.5 %collective-permute-start.23 = (f32[64,256]{1,0:T(8,128)S(1)}, f32[64,256]{1,0:T(8,128)S(1)}, u32[]{:S(2)}, u32[]{:S(2)}) collective-permute-start(f32[64,256]{1,0:T(8,128)S(1)} %get-tuple-element.62), channel_id=1, source_target_pairs={{0,7},{1,6},{2,5},{3,4},{4,3},{5,2},{6,1},{7,0},{8,15},{9,14},{10,... | collective-permute-start | bytes 196616 | tf_op jit(solution)/shard_map/ppermute | solution.py:546
  114.0 12.2 %collective-permute-start.24 = (f32[64,256]{1,0:T(8,128)S(1)}, f32[64,256]{1,0:T(8,128)S(1)}, u32[]{:S(2)}, u32[]{:S(2)}) collective-permute-start(f32[64,256]{1,0:T(8,128)S(1)} %get-tuple-element.63), channel_id=1, source_target_pairs={{0,8},{1,9},{2,10},{3,11},{4,12},{5,13},{6,14},{7,15},{8,0},{9,1},... | collective-permute-start | bytes 196616 | tf_op jit(solution)/shard_map/ppermute | solution.py:546
  116.0 12.9 %collective-permute-start.25 = (f32[64,256]{1,0:T(8,128)S(1)}, f32[64,256]{1,0:T(8,128)S(1)}, u32[]{:S(2)}, u32[]{:S(2)}) collective-permute-start(f32[64,256]{1,0:T(8,128)S(1)} %get-tuple-element.64), channel_id=1, source_target_pairs={{0,9},{1,8},{2,11},{3,10},{4,13},{5,12},{6,15},{7,14},{8,1},{9,0},... | collective-permute-start | bytes 196616 | tf_op jit(solution)/shard_map/ppermute | solution.py:546
  116.9 14.3 %collective-permute-start.26 = (f32[64,256]{1,0:T(8,128)S(1)}, f32[64,256]{1,0:T(8,128)S(1)}, u32[]{:S(2)}, u32[]{:S(2)}) collective-permute-start(f32[64,256]{1,0:T(8,128)S(1)} %get-tuple-element.65), channel_id=1, source_target_pairs={{0,10},{1,11},{2,8},{3,9},{4,14},{5,15},{6,12},{7,13},{8,2},{9,3},... | collective-permute-start | bytes 196616 | tf_op jit(solution)/shard_map/ppermute | solution.py:546
  119.0 16.4 %collective-permute-start.27 = (f32[64,256]{1,0:T(8,128)S(1)}, f32[64,256]{1,0:T(8,128)S(1)}, u32[]{:S(2)}, u32[]{:S(2)}) collective-permute-start(f32[64,256]{1,0:T(8,128)S(1)} %get-tuple-element.66), channel_id=1, source_target_pairs={{0,11},{1,10},{2,9},{3,8},{4,15},{5,14},{6,13},{7,12},{8,3},{9,2},... | collective-permute-start | bytes 196616 | tf_op jit(solution)/shard_map/ppermute | solution.py:546
  121.6 13.7 %collective-permute-start.28 = (f32[64,256]{1,0:T(8,128)S(1)}, f32[64,256]{1,0:T(8,128)S(1)}, u32[]{:S(2)}, u32[]{:S(2)}) collective-permute-start(f32[64,256]{1,0:T(8,128)S(1)} %get-tuple-element.67), channel_id=1, source_target_pairs={{0,12},{1,13},{2,14},{3,15},{4,8},{5,9},{6,10},{7,11},{8,4},{9,5},... | collective-permute-start | bytes 196616 | tf_op jit(solution)/shard_map/ppermute | solution.py:546
  126.2 9.1 %collective-permute-start.29 = (f32[64,256]{1,0:T(8,128)S(1)}, f32[64,256]{1,0:T(8,128)S(1)}, u32[]{:S(2)}, u32[]{:S(2)}) collective-permute-start(f32[64,256]{1,0:T(8,128)S(1)} %get-tuple-element.68), channel_id=1, source_target_pairs={{0,13},{1,12},{2,15},{3,14},{4,9},{5,8},{6,11},{7,10},{8,5},{9,4},... | collective-permute-start | bytes 196616 | tf_op jit(solution)/shard_map/ppermute | solution.py:546
  (27 other events, 503.9 us)
